TPU v7x, 256 devices: a whole 4x4x8 slice. The times are simulated.
256 devices in a mesh: sky: 32 (over x, z), band: 8 (over y, core).
Axes of the slice: x: 4, y: 4, z: 8, core: 2. Of those that a mesh axis runs over, the one named last changes fastest.
Arguments:
- residual_start: float32 [8, 32, 256, 256], P('band', 'sky'), may hold values from -6 to 6
- beam_pattern: float32 [8, 256, 256], P('band'), may hold values from -0.046875 to 0.046875
- spec_weights: float32 [8, 3], replicated, may hold values from -1 to 1
- thresholds: float32 [4, 3], replicated, may hold values from 0.3 to 1.5
- block_ids: int32 [8, 32, 4], P('band', 'sky'), may hold values from 0 to 3, each once within a row
- block_counts: int32 [8, 32], P('band', 'sky'), may hold values from 0 to 4, as said below
Outputs:
- model_coeffs: float32 [3, 32, 256, 256], P(None, 'sky', 'band')
- residual_final: float32 [8, 32, 256, 256], P('band', 'sky')
Inputs may be any that keep to these rules, and one draw needn't show every extreme that they name: `block_ids`: each list names every block of its tile once. `block_counts`: every subband has a tile with all 4 blocks occupied.
All inputs are finite; a program needn't handle non-finite values.
Results may differ from a plain program's by a relative error of at most 0.00014.
Values sent between devices are 32-bit elements; how exact they have to be, the bound alone decides.
A program may use at most 64 MiB of HBM per device.

v0:
```python
import math

import jax
import jax.numpy as jnp
from jax import lax
from jax.sharding import PartitionSpec as P

CYCLES = 2
TGX = 4


loop_gain = 0.25
highest = lax.Precision.HIGHEST


def shifted(x, axis, by):
    devices = lax.axis_size(axis)
    pairs = [(i, i + by) for i in range(devices) if 0 <= i + by < devices]
    return lax.ppermute(x, axis, pairs)


def matmul(left, right):
    return jnp.dot(left, right, precision=highest, preferred_element_type=jnp.float32)


def matmul_nt(left, right):
    return lax.dot_general(
        left, right, (((1,), (1,)), ((), ())), precision=highest, preferred_element_type=jnp.float32
    )


def smoothers(tile_cells, levels):
    position = jnp.arange(tile_cells, dtype=jnp.float32)
    offset = position[:, None] - position[None, :]
    stacked = []
    for scale_pos in range(levels):
        spread = 2.0**scale_pos * tile_cells / 16.0
        kernel = jnp.exp(-offset * offset / (2.0 * spread * spread))
        stacked.append(kernel / jnp.sqrt(jnp.sum(kernel * kernel, axis=1, keepdims=True)))
    return jnp.stack(stacked)


def fourier_tables(frame_size, inputs):
    wave_num = jnp.arange(frame_size, dtype=jnp.int32)[:, None]
    sample = jnp.arange(inputs, dtype=jnp.int32)[None, :]
    angles = (wave_num * sample % frame_size).astype(jnp.float32) * (2.0 * math.pi / frame_size)
    return (jnp.cos(angles), jnp.sin(angles))


def forward(values, cos_table, sin_table):
    by_cos = matmul(cos_table, values)
    by_sin = matmul(sin_table, values)
    real_part = matmul_nt(by_cos, cos_table) - matmul_nt(by_sin, sin_table)
    imag_part = -(matmul_nt(by_cos, sin_table) + matmul_nt(by_sin, cos_table))
    return (real_part, imag_part)


def backward(real_part, imag_part, cos_full, sin_full, frame_size):
    inv_real = matmul(cos_full, real_part) - matmul(sin_full, imag_part)
    inv_imag = matmul(sin_full, real_part) + matmul(cos_full, imag_part)
    return (matmul(inv_real, cos_full) - matmul(inv_imag, sin_full)) / float(
        frame_size * frame_size
    )


def on_device(residual_start, beam_pattern, spec_weights, thresholds, block_ids, block_counts):
    tile_cells = residual_start.shape[-1]
    half_tile = tile_cells // 2
    groups = lax.axis_size("band")
    slab_rows = tile_cells // groups
    band_pos = lax.axis_index("band")
    column_pos = lax.axis_index("sky") % TGX
    not_first = (column_pos != 0).astype(jnp.float32)
    not_last = (column_pos != TGX - 1).astype(jnp.float32)
    spread = beam_pattern.shape[-1]
    margin = spread // 2
    extent = tile_cells + spread
    inner_end = margin + tile_cells
    smooth = smoothers(tile_cells, thresholds.shape[0])
    own_smooth = lax.dynamic_slice_in_dim(smooth, band_pos * slab_rows, slab_rows, 1)
    own_weights = lax.dynamic_index_in_dim(spec_weights, band_pos, 0, keepdims=False)
    ids_row = block_ids[0, 0]
    live_count = block_counts[0, 0]
    frame_size = half_tile + spread
    cos_in, sin_in = fourier_tables(frame_size, half_tile)
    cos_psf, sin_psf = fourier_tables(frame_size, spread)
    cos_out, sin_out = fourier_tables(frame_size, frame_size)
    beam_re, beam_im = forward(beam_pattern[0], cos_psf, sin_psf)

    def neighbour(piece_vals, offset):
        return shifted(piece_vals, "sky", offset)

    coef_count = spec_weights.shape[1]
    level_count = thresholds.shape[0]
    residual = residual_start[0, 0]
    model_rows = jnp.zeros((coef_count, slab_rows, tile_cells), jnp.float32)
    for cycle_pos in range(CYCLES):
        partial_value = own_weights[:, None, None] * residual[None]
        spectral = lax.psum_scatter(partial_value, "band", scatter_dimension=1, tiled=True)
        vertical = jnp.einsum(
            "jrn,knx->jkrx",
            own_smooth,
            lax.all_gather(spectral, "band", axis=1, tiled=True),
            precision=highest,
            preferred_element_type=jnp.float32,
        )
        update = jnp.zeros((coef_count, slab_rows, tile_cells), jnp.float32)
        for scale_pos in range(level_count):
            smoothed = jnp.einsum(
                "kri,xi->krx",
                vertical[scale_pos],
                smooth[scale_pos],
                precision=highest,
                preferred_element_type=jnp.float32,
            )
            cutoff = thresholds[scale_pos][:, None, None]
            update = update + smoothed - jnp.clip(smoothed, -cutoff, cutoff)
        update = loop_gain * update
        model_rows = model_rows + update
        gathered = lax.all_gather(update, "band", axis=1, tiled=True)
        sub_image = jnp.einsum(
            "k,kyx->yx",
            own_weights,
            gathered,
            precision=highest,
            preferred_element_type=jnp.float32,
        )

        def add_block(slot_pos, canvas):
            block_pos = ids_row[slot_pos]
            top_row = block_pos // 2 * half_tile
            left_col = block_pos % 2 * half_tile
            block_vals = lax.dynamic_slice(sub_image, (top_row, left_col), (half_tile, half_tile))
            real_part, imag_part = forward(block_vals, cos_in, sin_in)
            prod_real = real_part * beam_re - imag_part * beam_im
            prod_imag = real_part * beam_im + imag_part * beam_re
            footprint = backward(prod_real, prod_imag, cos_out, sin_out, frame_size)
            current = lax.dynamic_slice(canvas, (top_row, left_col), (frame_size, frame_size))
            return lax.dynamic_update_slice(canvas, current + footprint, (top_row, left_col))

        settle_canvas = lax.fori_loop(
            0, live_count, add_block, jnp.zeros((extent, extent), jnp.float32)
        )
        low_end = tile_cells - margin
        interior = settle_canvas[margin:inner_end, margin:inner_end]
        interior = interior.at[:, :margin].add(
            not_first * neighbour(settle_canvas[margin:inner_end, inner_end:], 1)
        )
        interior = interior.at[:, low_end:].add(
            not_last * neighbour(settle_canvas[margin:inner_end, :margin], -1)
        )
        interior = interior.at[:margin, :].add(
            neighbour(settle_canvas[inner_end:, margin:inner_end], TGX)
        )
        interior = interior.at[low_end:, :].add(
            neighbour(settle_canvas[:margin, margin:inner_end], -TGX)
        )
        interior = interior.at[:margin, :margin].add(
            not_first * neighbour(settle_canvas[inner_end:, inner_end:], TGX + 1)
        )
        interior = interior.at[:margin, low_end:].add(
            not_last * neighbour(settle_canvas[inner_end:, :margin], TGX - 1)
        )
        interior = interior.at[low_end:, :margin].add(
            not_first * neighbour(settle_canvas[:margin, inner_end:], 1 - TGX)
        )
        interior = interior.at[low_end:, low_end:].add(
            not_last * neighbour(settle_canvas[:margin, :margin], -TGX - 1)
        )
        residual = residual - interior
    return (model_rows[:, None], residual[None, None])


def solution(mesh):
    placed = (
        P("band", "sky", None, None),
        P("band", None, None),
        P(),
        P(),
        P("band", "sky", None),
        P("band", "sky"),
    )
    return jax.shard_map(
        on_device,
        mesh=mesh,
        in_specs=placed,
        out_specs=(P(None, "sky", "band", None), P("band", "sky", None, None)),
        check_vma=False,
    )
```

profile of v0, /device:TPU:6, one launch (start us, length us, event | category | flops | bytes accessed | tf_op | source)
XLA Modules:
  0.0 618.1 jit_solution(16205080069021389443)
XLA Ops:
  28.3 19.5 %reduce-scatter.3.cloned.1.call-done = f32[3,32,256]{2,1,0:T(8,128)} async-done(((f32[3,256,256]{2,1,0:T(8,128)}), f32[3,32,256]{2,1,0:T(8,128)}) %reduce-scatter.3.cloned.1.call-update) | async-done | bytes 98320 | tf_op jit(solution)/shard_map/reduce_scatter | solution.py:99
  47.7 14.0 %all_gather.12 = f32[3,256,256]{2,1,0:T(8,128)S(1)} all-gather(f32[3,32,256]{2,1,0:T(8,128)} %reduce-scatter.3.cloned.1.call-done), channel_id=1, replica_groups=mesh['sky'=32,'band'=8] {'band'}, dimensions={1}, use_global_device_ids=true | all-gather | bytes 884736 | tf_op jit(solution)/shard_map/all_gather | solution.py:103
  64.2 13.4 %all_gather.13 = f32[3,256,256]{2,1,0:T(8,128)S(1)} all-gather(f32[3,32,256]{2,1,0:T(8,128)S(1)} %subtract_multiply_fusion.1), channel_id=1, replica_groups=mesh['sky'=32,'band'=8] {'band'}, dimensions={1}, use_global_device_ids=true | all-gather | bytes 884736 | tf_op jit(solution)/shard_map/all_gather | solution.py:120
  80.4 171.7 %while.44 = (s32[]{:T(128)}, f32[512,512]{1,0:T(8,128)S(1)}, s32[]{:T(128)}, s32[4]{0:T(128)S(1)}, f32[256,256]{1,0:T(8,128)S(1)}, /*index=5*/f32[384,384]{1,0:T...) while((s32[]{:T(128)}, f32[512,512]{1,0:T(8,128)S(1)}, ...), condition=%wide.region_6.7_spmd.clone.clone, body=%wide.region_5.6_spmd.clone.clone.sunk | while | flops 5146509312 | bytes 16646692 | solution.py:141
  114.5 4.2 fusion.505
  118.7 4.1 fusion.503
  122.8 4.2 convolution_subtract_fusion.12
  127.0 4.1 convolution_add_fusion.7
  150.4 4.2 fusion.505
  154.6 4.1 fusion.503
  158.7 4.2 convolution_subtract_fusion.12
  162.8 4.1 convolution_add_fusion.7
  186.2 4.2 fusion.505
  194.5 4.2 convolution_subtract_fusion.12
  198.7 4.1 convolution_add_fusion.7
  222.1 4.2 fusion.505
  230.4 4.2 convolution_subtract_fusion.12
  234.5 4.1 convolution_add_fusion.7
  256.0 6.3 %collective-permute-start.4 = (f32[128,128]{1,0:T(8,128)S(1)}, f32[128,128]{1,0:T(8,128)S(1)}, u32[]{:S(2)}, u32[]{:S(2)}) collective-permute-start(f32[128,128]{1,0:T(8,128)S(1)} %get-tuple-element.694), channel_id=1, source_target_pairs={{0,40},{8,48},{16,56},{24,64},{32,72},{40,80},{48,88},{56,96},{64,... | collective-permute-start | bytes 196616 | tf_op jit(solution)/shard_map/ppermute | solution.py:19
  262.4 8.5 %collective-permute-start.6 = (f32[128,128]{1,0:T(8,128)S(1)}, f32[128,128]{1,0:T(8,128)S(1)}, u32[]{:S(2)}, u32[]{:S(2)}) collective-permute-start(f32[128,128]{1,0:T(8,128)S(1)} %get-tuple-element.695), channel_id=1, source_target_pairs={{24,0},{32,8},{40,16},{48,24},{56,32},{64,40},{72,48},{80,56},{88,... | collective-permute-start | bytes 196616 | tf_op jit(solution)/shard_map/ppermute | solution.py:19
  274.3 5.5 collective-permute-done
  282.4 4.3 collective-permute-done.1
  288.6 11.1 %collective-permute-done.2 = f32[128,256]{1,0:T(8,128)S(1)} collective-permute-done((f32[128,256]{1,0:T(8,128)S(1)}, f32[128,256]{1,0:T(8,128)S(1)}, u32[]{:S(2)}, u32[]{:S(2)}) %collective-permute-start.2) | collective-permute-done | bytes 131104 | tf_op jit(solution)/shard_map/ppermute | solution.py:19
  299.7 6.4 %collective-permute-start.3 = (f32[128,256]{1,0:T(8,128)S(1)}, f32[128,256]{1,0:T(8,128)S(1)}, u32[]{:S(2)}, u32[]{:S(2)}) collective-permute-start(f32[128,256]{1,0:T(8,128)S(1)} %get-tuple-element.696), channel_id=1, source_target_pairs={{32,0},{40,8},{48,16},{56,24},{64,32},{72,40},{80,48},{88,56},{96,... | collective-permute-start | bytes 393224 | tf_op jit(solution)/shard_map/ppermute | solution.py:19
  306.1 5.0 collective-permute-done.3
  316.8 32.0 %reduce-scatter.5.cloned.1.call-done = f32[3,32,256]{2,1,0:T(8,128)} async-done(((f32[3,256,256]{2,1,0:T(8,128)}), f32[3,32,256]{2,1,0:T(8,128)}) %reduce-scatter.5.cloned.1.call-update) | async-done | bytes 98320 | tf_op jit(solution)/shard_map/reduce_scatter | solution.py:99
  348.8 13.6 %all_gather.14 = f32[3,256,256]{2,1,0:T(8,128)S(1)} all-gather(f32[3,32,256]{2,1,0:T(8,128)} %reduce-scatter.5.cloned.1.call-done), channel_id=1, replica_groups=mesh['sky'=32,'band'=8] {'band'}, dimensions={1}, use_global_device_ids=true | all-gather | bytes 884736 | tf_op jit(solution)/shard_map/all_gather | solution.py:103
  364.9 13.4 %all_gather.15 = f32[3,256,256]{2,1,0:T(8,128)S(1)} all-gather(f32[3,32,256]{2,1,0:T(8,128)S(1)} %subtract_multiply_fusion), channel_id=1, replica_groups=mesh['sky'=32,'band'=8] {'band'}, dimensions={1}, use_global_device_ids=true | all-gather | bytes 884736 | tf_op jit(solution)/shard_map/all_gather | solution.py:120
  380.6 166.0 %while.45 = (s32[]{:T(128)}, f32[512,512]{1,0:T(8,128)S(1)}, s32[]{:T(128)}, s32[4]{0:T(128)S(1)}, f32[256,256]{1,0:T(8,128)S(1)}, /*index=5*/f32[384,384]{1,0:T...) while((s32[]{:T(128)}, f32[512,512]{1,0:T(8,128)S(1)}, ...), condition=%wide.region_11.12_spmd.clone.clone, body=%wide.region_10.11_spmd.clone.clone.sunk | while | flops 5146509312 | bytes 16646692 | solution.py:141
  414.5 4.2 fusion.536
  422.8 4.2 convolution_subtract_fusion.14
  427.0 4.1 convolution_add_fusion.8
  450.4 4.2 fusion.536
  458.7 4.2 convolution_subtract_fusion.14
  462.8 4.1 convolution_add_fusion.8
  486.2 4.2 fusion.536
  494.5 4.2 convolution_subtract_fusion.14
  498.7 4.1 convolution_add_fusion.8
  522.1 4.2 fusion.536
  530.4 4.2 convolution_subtract_fusion.14
  534.5 4.1 convolution_add_fusion.8
  550.6 6.3 %collective-permute-start.12 = (f32[128,128]{1,0:T(8,128)S(1)}, f32[128,128]{1,0:T(8,128)S(1)}, u32[]{:S(2)}, u32[]{:S(2)}) collective-permute-start(f32[128,128]{1,0:T(8,128)S(1)} %get-tuple-element.686), channel_id=1, source_target_pairs={{0,40},{8,48},{16,56},{24,64},{32,72},{40,80},{48,88},{56,96},{64,... | collective-permute-start | bytes 196616 | tf_op jit(solution)/shard_map/ppermute | solution.py:19
  556.9 8.5 %collective-permute-start.14 = (f32[128,128]{1,0:T(8,128)S(1)}, f32[128,128]{1,0:T(8,128)S(1)}, u32[]{:S(2)}, u32[]{:S(2)}) collective-permute-start(f32[128,128]{1,0:T(8,128)S(1)} %get-tuple-element.687), channel_id=1, source_target_pairs={{24,0},{32,8},{40,16},{48,24},{56,32},{64,40},{72,48},{80,56},{88,... | collective-permute-start | bytes 196616 | tf_op jit(solution)/shard_map/ppermute | solution.py:19
  569.5 4.8 collective-permute-done.8
  576.9 4.3 collective-permute-done.9
  583.1 11.1 %collective-permute-done.10 = f32[128,256]{1,0:T(8,128)S(1)} collective-permute-done((f32[128,256]{1,0:T(8,128)S(1)}, f32[128,256]{1,0:T(8,128)S(1)}, u32[]{:S(2)}, u32[]{:S(2)}) %collective-permute-start.10) | collective-permute-done | bytes 131104 | tf_op jit(solution)/shard_map/ppermute | solution.py:19
  594.3 6.4 %collective-permute-start.11 = (f32[128,256]{1,0:T(8,128)S(1)}, f32[128,256]{1,0:T(8,128)S(1)}, u32[]{:S(2)}, u32[]{:S(2)}) collective-permute-start(f32[128,256]{1,0:T(8,128)S(1)} %get-tuple-element.688), channel_id=1, source_target_pairs={{32,0},{40,8},{48,16},{56,24},{64,32},{72,40},{80,48},{88,56},{96,... | collective-permute-start | bytes 393224 | tf_op jit(solution)/shard_map/ppermute | solution.py:19
  600.7 4.9 collective-permute-done.11
  (181 shorter events, 218.9 us)
Async XLA Ops:
  7.2 6.7 %copy-start = (f32[1,256,256]{2,1,0:T(8,128)S(1)}, f32[1,256,256]{2,1,0:T(8,128)}, u32[]{:S(2)}) copy-start(f32[1,256,256]{2,1,0:T(8,128)} %param.43) | copy-start | bytes 786436
  7.2 40.6 %reduce-scatter.3.cloned.1.call-start = ((), (), s32[]{:S(2)}) async-start(), calls=%async_computation.2 | async-start | bytes 884736 | tf_op jit(solution)/shard_map/reduce_scatter | solution.py:99
  7.2 0.7 copy-start.3
  10.1 338.7 %reduce-scatter.5.cloned.1.call-start = ((), (), s32[]{:S(2)}) async-start(), calls=%async_computation.3 | async-start | bytes 884736 | tf_op jit(solution)/shard_map/reduce_scatter | solution.py:99
  12.1 0.7 copy-start.2
  79.8 0.7 copy-start.4
  252.2 63.4 %collective-permute-start.7 = (f32[128,128]{1,0:T(8,128)S(1)}, f32[128,128]{1,0:T(8,128)S(1)}, u32[]{:S(2)}, u32[]{:S(2)}) collective-permute-start(f32[128,128]{1,0:T(8,128)S(1)} %get-tuple-element.692), channel_id=1, source_target_pairs={{40,0},{48,8},{56,16},{64,24},{72,32},{80,40},{88,48},{96,56},{104... | collective-permute-start | bytes 196616 | tf_op jit(solution)/shard_map/ppermute | solution.py:19
  254.1 57.0 %collective-permute-start.5 = (f32[128,128]{1,0:T(8,128)S(1)}, f32[128,128]{1,0:T(8,128)S(1)}, u32[]{:S(2)}, u32[]{:S(2)}) collective-permute-start(f32[128,128]{1,0:T(8,128)S(1)} %get-tuple-element.693), channel_id=1, source_target_pairs={{0,24},{8,32},{16,40},{24,48},{32,56},{40,64},{48,72},{56,80},{64,... | collective-permute-start | bytes 196616 | tf_op jit(solution)/shard_map/ppermute | solution.py:19
  256.0 55.1 %collective-permute-start.4 = (f32[128,128]{1,0:T(8,128)S(1)}, f32[128,128]{1,0:T(8,128)S(1)}, u32[]{:S(2)}, u32[]{:S(2)}) collective-permute-start(f32[128,128]{1,0:T(8,128)S(1)} %get-tuple-element.694), channel_id=1, source_target_pairs={{0,40},{8,48},{16,56},{24,64},{32,72},{40,80},{48,88},{56,96},{64,... | collective-permute-start | bytes 196616 | tf_op jit(solution)/shard_map/ppermute | solution.py:19
  262.4 53.2 %collective-permute-start.6 = (f32[128,128]{1,0:T(8,128)S(1)}, f32[128,128]{1,0:T(8,128)S(1)}, u32[]{:S(2)}, u32[]{:S(2)}) collective-permute-start(f32[128,128]{1,0:T(8,128)S(1)} %get-tuple-element.695), channel_id=1, source_target_pairs={{24,0},{32,8},{40,16},{48,24},{56,32},{64,40},{72,48},{80,56},{88,... | collective-permute-start | bytes 196616 | tf_op jit(solution)/shard_map/ppermute | solution.py:19
  270.8 9.0 %collective-permute-start = (f32[256,128]{1,0:T(8,128)S(1)}, f32[256,128]{1,0:T(8,128)S(1)}, u32[]{:S(2)}, u32[]{:S(2)}) collective-permute-start(f32[256,128]{1,0:T(8,128)S(1)} %get-tuple-element.699), channel_id=1, source_target_pairs={{0,8},{8,16},{16,24},{24,32},{32,40},{40,48},{48,56},{56,64},{64,7... | collective-permute-start | bytes 393224 | tf_op jit(solution)/shard_map/ppermute | solution.py:19
  279.8 6.8 %collective-permute-start.1 = (f32[256,128]{1,0:T(8,128)S(1)}, f32[256,128]{1,0:T(8,128)S(1)}, u32[]{:S(2)}, u32[]{:S(2)}) collective-permute-start(f32[256,128]{1,0:T(8,128)S(1)} %get-tuple-element.698), channel_id=1, source_target_pairs={{8,0},{16,8},{24,16},{32,24},{40,32},{48,40},{56,48},{64,56},{72,6... | collective-permute-start | bytes 393224 | tf_op jit(solution)/shard_map/ppermute | solution.py:19
  286.6 13.1 %collective-permute-start.2 = (f32[128,256]{1,0:T(8,128)S(1)}, f32[128,256]{1,0:T(8,128)S(1)}, u32[]{:S(2)}, u32[]{:S(2)}) collective-permute-start(f32[128,256]{1,0:T(8,128)S(1)} %get-tuple-element.697), channel_id=1, source_target_pairs={{0,32},{8,40},{16,48},{24,56},{32,64},{40,72},{48,80},{56,88},{64,... | collective-permute-start | bytes 393224 | tf_op jit(solution)/shard_map/ppermute | solution.py:19
  299.7 11.4 %collective-permute-start.3 = (f32[128,256]{1,0:T(8,128)S(1)}, f32[128,256]{1,0:T(8,128)S(1)}, u32[]{:S(2)}, u32[]{:S(2)}) collective-permute-start(f32[128,256]{1,0:T(8,128)S(1)} %get-tuple-element.696), channel_id=1, source_target_pairs={{32,0},{40,8},{48,16},{56,24},{64,32},{72,40},{80,48},{88,56},{96,... | collective-permute-start | bytes 393224 | tf_op jit(solution)/shard_map/ppermute | solution.py:19
  313.1 2.5 copy-start.1
  546.7 63.4 %collective-permute-start.15 = (f32[128,128]{1,0:T(8,128)S(1)}, f32[128,128]{1,0:T(8,128)S(1)}, u32[]{:S(2)}, u32[]{:S(2)}) collective-permute-start(f32[128,128]{1,0:T(8,128)S(1)} %get-tuple-element.684), channel_id=1, source_target_pairs={{40,0},{48,8},{56,16},{64,24},{72,32},{80,40},{88,48},{96,56},{104... | collective-permute-start | bytes 196616 | tf_op jit(solution)/shard_map/ppermute | solution.py:19
  548.7 57.0 %collective-permute-start.13 = (f32[128,128]{1,0:T(8,128)S(1)}, f32[128,128]{1,0:T(8,128)S(1)}, u32[]{:S(2)}, u32[]{:S(2)}) collective-permute-start(f32[128,128]{1,0:T(8,128)S(1)} %get-tuple-element.685), channel_id=1, source_target_pairs={{0,24},{8,32},{16,40},{24,48},{32,56},{40,64},{48,72},{56,80},{64,... | collective-permute-start | bytes 196616 | tf_op jit(solution)/shard_map/ppermute | solution.py:19
  550.6 55.1 %collective-permute-start.12 = (f32[128,128]{1,0:T(8,128)S(1)}, f32[128,128]{1,0:T(8,128)S(1)}, u32[]{:S(2)}, u32[]{:S(2)}) collective-permute-start(f32[128,128]{1,0:T(8,128)S(1)} %get-tuple-element.686), channel_id=1, source_target_pairs={{0,40},{8,48},{16,56},{24,64},{32,72},{40,80},{48,88},{56,96},{64,... | collective-permute-start | bytes 196616 | tf_op jit(solution)/shard_map/ppermute | solution.py:19
  556.9 53.2 %collective-permute-start.14 = (f32[128,128]{1,0:T(8,128)S(1)}, f32[128,128]{1,0:T(8,128)S(1)}, u32[]{:S(2)}, u32[]{:S(2)}) collective-permute-start(f32[128,128]{1,0:T(8,128)S(1)} %get-tuple-element.687), channel_id=1, source_target_pairs={{24,0},{32,8},{40,16},{48,24},{56,32},{64,40},{72,48},{80,56},{88,... | collective-permute-start | bytes 196616 | tf_op jit(solution)/shard_map/ppermute | solution.py:19
  565.4 9.0 %collective-permute-start.8 = (f32[256,128]{1,0:T(8,128)S(1)}, f32[256,128]{1,0:T(8,128)S(1)}, u32[]{:S(2)}, u32[]{:S(2)}) collective-permute-start(f32[256,128]{1,0:T(8,128)S(1)} %get-tuple-element.691), channel_id=1, source_target_pairs={{0,8},{8,16},{16,24},{24,32},{32,40},{40,48},{48,56},{56,64},{64,7... | collective-permute-start | bytes 393224 | tf_op jit(solution)/shard_map/ppermute | solution.py:19
  574.3 6.8 %collective-permute-start.9 = (f32[256,128]{1,0:T(8,128)S(1)}, f32[256,128]{1,0:T(8,128)S(1)}, u32[]{:S(2)}, u32[]{:S(2)}) collective-permute-start(f32[256,128]{1,0:T(8,128)S(1)} %get-tuple-element.690), channel_id=1, source_target_pairs={{8,0},{16,8},{24,16},{32,24},{40,32},{48,40},{56,48},{64,56},{72,6... | collective-permute-start | bytes 393224 | tf_op jit(solution)/shard_map/ppermute | solution.py:19
  581.2 13.1 %collective-permute-start.10 = (f32[128,256]{1,0:T(8,128)S(1)}, f32[128,256]{1,0:T(8,128)S(1)}, u32[]{:S(2)}, u32[]{:S(2)}) collective-permute-start(f32[128,256]{1,0:T(8,128)S(1)} %get-tuple-element.689), channel_id=1, source_target_pairs={{0,32},{8,40},{16,48},{24,56},{32,64},{40,72},{48,80},{56,88},{64,... | collective-permute-start | bytes 393224 | tf_op jit(solution)/shard_map/ppermute | solution.py:19
  594.3 11.4 %collective-permute-start.11 = (f32[128,256]{1,0:T(8,128)S(1)}, f32[128,256]{1,0:T(8,128)S(1)}, u32[]{:S(2)}, u32[]{:S(2)}) collective-permute-start(f32[128,256]{1,0:T(8,128)S(1)} %get-tuple-element.688), channel_id=1, source_target_pairs={{32,0},{40,8},{48,16},{56,24},{64,32},{72,40},{80,48},{88,56},{96,... | collective-permute-start | bytes 393224 | tf_op jit(solution)/shard_map/ppermute | solution.py:19
Sparse Core Ops, SparseCore 0:
  10.5 37.1 reduce-scatter.2
  316.9 31.8 reduce-scatter.4
where the time goes:
time: 620 us; the launch traced here: 618 us
  matrix products  279 us (45%)
  waiting for transfers between devices  102 us (16%)
  loops' own time  77.2 us (12%)
  starting transfers between devices  64.7 us (10%)
  blocking collectives  54.4 us (9%)
  between operations  15.1 us (2%)
  local copies, waits for them, and re-layouts  13 us (2%)
  other arithmetic  12.4 us (2%)
    dot_general x66, matrix products, matmul(): jnp.dot(left, right, precision=highest, preferred_element_type=jnp.float32)  212 us
    another operation x2, loops' own time, on_device(): lax.fori_loop(0, live_count, add_block, jnp.zeros((extent, extent), jnp.f...  77.2 us
    ppermute x16, starting transfers between devices, shifted(): return lax.ppermute(x, axis, pairs)  64.6 us
    dot_general x36, matrix products, matmul_nt(): lax.dot_general(left, right, (((1,), (1,)), ((), ())), precision=highest,...  57.2 us
    reduce_scatter x2, waiting for transfers between devices, on_device(): lax.psum_scatter(partial_value, 'band', scatter_dimension=1, tiled=True)  51.5 us
    ppermute x16, waiting for transfers between devices, shifted(): return lax.ppermute(x, axis, pairs)  50.9 us
    all_gather x2, blocking collectives, on_device(): lax.all_gather(spectral, 'band', axis=1, tiled=True)  27.6 us
    all_gather x2, blocking collectives, on_device(): gathered = lax.all_gather(update, 'band', axis=1, tiled=True)  26.8 us
  transfers between devices with their start and end apart: 18, of which 10 were waited for; matrix products, arithmetic and copies ran while one was open for 5% of the time, Pallas kernels for 0%

commit v1 on v0

v1 whole, which is shorter than its diff:
```python
import functools

import jax
import jax.numpy as jnp
import numpy as np
from jax import lax
from jax.experimental import pallas as pl
from jax.experimental.pallas import tpu as pltpu
from jax.sharding import PartitionSpec as P

CYCLES = 2
TGX = 4
GAIN = 0.25
RANK = 42
KPAD = 48
FLAG_ROW = 44
MESH = pl.DeviceIdType.MESH
BF = jnp.bfloat16
F32 = jnp.float32


def host_split(a):
    hi = np.asarray(a, np.float64).astype(BF)
    lo = (np.asarray(a, np.float64) - hi.astype(np.float64)).astype(BF)
    return hi, lo


def host_tables(tile, levels):
    pos = np.arange(tile, dtype=np.float64)
    off = pos[:, None] - pos[None, :]
    smooth = []
    for j in range(levels):
        spread = 2.0**j * tile / 16.0
        k = np.exp(-off * off / (2.0 * spread * spread))
        smooth.append(k / np.sqrt(np.sum(k * k, axis=1, keepdims=True)))
    smooth = np.stack(smooth)
    _, _, vt = np.linalg.svd(smooth.reshape(-1, tile), full_matrices=False)
    basis = vt[:RANK].T
    proj = np.zeros((tile, 128))
    proj[:, :RANK] = basis
    proj_t = np.zeros((KPAD, tile))
    proj_t[:RANK] = basis.T
    expand = smooth @ basis
    half = tile // 2

    p_hi, p_lo = host_split(proj)
    t_hi, t_lo = host_split(proj_t)
    project = np.concatenate([p_hi, p_hi, p_lo], axis=0)
    project_t = np.concatenate([t_hi, t_hi, t_lo], axis=1)

    left = np.zeros((levels, tile, KPAD))
    left[:, :, :RANK] = expand
    l_hi, l_lo = host_split(left)
    left3 = np.concatenate([l_hi, l_hi, l_lo], axis=2)

    right = np.zeros((levels, 128, 6 * half))
    for k in range(3):
        for h in range(2):
            at = (3 * h + k) * half
            right[:, RANK * k : RANK * (k + 1), at : at + half] = expand[
                :, h * half : (h + 1) * half
            ].transpose(0, 2, 1)
    r_hi, r_lo = host_split(right)
    right3 = np.concatenate([r_hi, r_lo], axis=1)

    n = 2 * tile
    f = np.arange(tile) + 0.5
    samp = np.arange(n)
    ang = 2.0 * np.pi * f[:, None] * samp[None, :] / n
    rows_f = np.concatenate([np.cos(ang), -np.sin(ang)], axis=0)
    f_hi, f_lo = host_split(rows_f)
    rows_fwd = np.stack([f_hi, f_lo])
    ang_out = ang[:, tile:].T
    rows_i = np.concatenate([np.cos(ang_out), -np.sin(ang_out)], axis=1) * (2.0 / (n * n))
    i_hi, i_lo = host_split(rows_i)
    rows_inv = np.stack([i_hi, i_lo])

    fwd, inv = [], []
    x = np.arange(tile)
    for parity in range(2):
        a = 2.0 * np.pi * x[:, None] * (2 * np.arange(tile)[None, :] + parity) / n
        c, s = np.cos(a), np.sin(a)
        sign = 1.0 - 2.0 * parity
        fwd.append(np.stack(host_split(np.concatenate([c, s], axis=0))))
        inv.append(np.stack(host_split(sign * np.concatenate([c.T, s.T], axis=0))))
    cols_fwd, cols_inv = np.stack(fwd), np.stack(inv)
    return project, project_t, left3, right3, rows_fwd, rows_inv, cols_fwd, cols_inv


def split(v):
    hi = v.astype(BF)
    return hi, (v - hi.astype(F32)).astype(BF)


def dot(a, b):
    return jnp.dot(a, b, preferred_element_type=F32)


def data_const(hi, lo, c_hi, c_lo):
    return dot(jnp.concatenate([hi, lo, hi], axis=1), jnp.concatenate([c_hi, c_hi, c_lo], axis=0))


def const_data(c_hi, c_lo, hi, lo):
    return dot(jnp.concatenate([c_hi, c_hi, c_lo], axis=1), jnp.concatenate([hi, lo, hi], axis=0))


def soft(v, t):
    return v - jnp.minimum(jnp.maximum(v, -t), t)


def rotate(hi, lo):
    half = hi.shape[0] // 2

    def one(v):
        return jnp.concatenate(
            [
                jnp.concatenate([v[:half], v[half:]], axis=1),
                jnp.concatenate([v[half:], -v[:half]], axis=1),
            ],
            axis=0,
        )

    return one(hi), one(lo)


SLOTS = [(dr, dc) for dr in (-1, 0, 1) for dc in (-1, 0, 1)]


def kernel(
    bands,
    sky,
    ids_ref,
    count_ref,
    weight_ref,
    thr_ref,
    res_in,
    beam_ref,
    project_hbm,
    project_t_hbm,
    left_hbm,
    right_hbm,
    rows_fwd_hbm,
    rows_inv_hbm,
    cols_fwd_hbm,
    cols_inv_hbm,
    model_out,
    res_out,
    project,
    project_t,
    left,
    right,
    rows_fwd,
    rows_inv,
    cols_fwd,
    cols_inv,
    gather,
    sky_buf,
    coef3,
    own3,
    u_hi,
    u_lo,
    win,
    win_hi,
    win_lo,
    beam_f,
    sd_hi,
    sd_lo,
    z_acc,
    const_sem,
    band_send,
    band_recv,
    sky_send,
    sky_recv,
):
    tile = res_in.shape[0]
    half = tile // 2
    levels = left.shape[0]
    slab = tile // bands
    sky_rows = sky // TGX
    me = lax.axis_index("band")
    spot = lax.axis_index("sky")
    row, col = spot // TGX, spot % TGX

    def sky_id(dr, dc):
        return ((row + dr + sky_rows) % sky_rows) * TGX + (col + dc + TGX) % TGX

    pairs = [
        (project_t_hbm, project_t),
        (project_hbm, project),
        (rows_fwd_hbm, rows_fwd),
        (cols_fwd_hbm, cols_fwd),
        (left_hbm, left),
        (right_hbm, right),
        (cols_inv_hbm, cols_inv),
        (rows_inv_hbm, rows_inv),
    ]
    copies = [
        pltpu.make_async_copy(src, dst, const_sem.at[i]) for i, (src, dst) in enumerate(pairs)
    ]
    for copy in copies:
        copy.start()

    barrier = pltpu.get_barrier_semaphore()
    for d in range(1, bands):
        pl.semaphore_signal(
            barrier, inc=1, device_id={"band": (me + d) % bands}, device_id_type=MESH
        )
    for dr, dc in SLOTS:
        if (dr, dc) != (0, 0):
            pl.semaphore_signal(
                barrier, inc=1, device_id={"sky": sky_id(dr, dc)}, device_id_type=MESH
            )
    pl.semaphore_wait(barrier, bands - 1 + 8)

    res_out[...] = res_in[...]
    model_out[...] = jnp.zeros_like(model_out)
    copies[0].wait()
    copies[1].wait()

    lane = lax.broadcasted_iota(jnp.int32, (1, 128), 1)
    lane16 = lax.broadcasted_iota(jnp.int32, (16, 128), 1)
    row48 = lax.broadcasted_iota(jnp.int32, (KPAD, 128), 0)
    flags = []
    for q in range(4):
        live = jnp.float32(0.0)
        for s in range(4):
            hit = jnp.where(ids_ref[s] == q, 1.0, 0.0) * jnp.where(s < count_ref[0], 1.0, 0.0)
            live = live + hit
        flags.append(live)
    weights = [weight_ref[me, k] for k in range(3)]
    scale = jnp.zeros((1, 128), F32)
    for k in range(3):
        inside = (lane >= RANK * k) & (lane < RANK * (k + 1))
        scale = jnp.where(inside, GAIN * weights[k], scale)

    def band_copy(cyc, d):
        return pltpu.make_async_remote_copy(
            src_ref=gather.at[cyc, 0],
            dst_ref=gather.at[cyc, d],
            send_sem=band_send.at[cyc, d],
            recv_sem=band_recv.at[cyc, d],
            device_id={"band": (me + d) % bands},
            device_id_type=MESH,
        )

    def sky_copy(cyc, dr, dc):
        slot = (1 - dr) * 3 + (1 - dc)
        return pltpu.make_async_remote_copy(
            src_ref=sky_buf.at[cyc, 4],
            dst_ref=sky_buf.at[cyc, slot],
            send_sem=sky_send.at[cyc, slot],
            recv_sem=sky_recv.at[cyc, slot],
            device_id={"sky": sky_id(dr, dc)},
            device_id_type=MESH,
        )

    def valid(dr, dc):
        good = (row + dr >= 0) & (row + dr < sky_rows) & (col + dc >= 0) & (col + dc < TGX)
        return jnp.where(good, 1.0, 0.0)

    def cycle(cyc, carry):
        r_hi, r_lo = split(res_out[...])
        part = dot(project_t[...], jnp.concatenate([r_hi, r_lo, r_hi], axis=0))
        p_hi, p_lo = split(part)
        coef = dot(jnp.concatenate([p_hi, p_lo, p_hi], axis=1), project[...])
        gather[cyc, 0] = (
            coef[0:16]
            + pltpu.roll(coef[16:32], RANK, 1)
            + pltpu.roll(coef[32:48], 2 * RANK, 1)
        )
        for d in range(1, bands):
            band_copy(cyc, d).start()

        @pl.when(cyc == 0)
        def _():
            copies[2].wait()
            copies[3].wait()
            b_hi, b_lo = split(beam_ref[...])
            first = const_data(rows_fwd[0, :, :tile], rows_fwd[1, :, :tile], b_hi, b_lo)
            l_hi, l_lo = rotate(*split(first))
            for parity in range(2):
                beam_f[parity] = data_const(l_hi, l_lo, cols_fwd[parity, 0], cols_fwd[parity, 1])
            copies[4].wait()
            copies[5].wait()

        for d in range(1, bands):
            band_copy(cyc, d).wait_recv()
        sums = []
        for k in range(3):
            total = weights[k] * gather[cyc, 0]
            for d in range(1, bands):
                total = total + weight_ref[(me - d + bands) % bands, k] * gather[cyc, d]
            sums.append(total)
        groups = []
        for g in range(3):
            out = jnp.zeros((16, 128), F32)
            for k in range(3):
                moved = sums[k]
                if k != g:
                    moved = pltpu.roll(moved, (RANK * (k - g)) % 128, 1)
                inside = (lane16 >= RANK * k) & (lane16 < RANK * (k + 1))
                out = jnp.where(inside, moved, out)
            groups.append(out)
        full = jnp.concatenate(groups, axis=0)
        for q in range(4):
            full = jnp.where(row48 == FLAG_ROW + q, flags[q], full)
        sky_buf[cyc, 4] = full
        for dr, dc in SLOTS:
            if (dr, dc) != (0, 0):
                sky_copy(cyc, dr, dc).start()

        o_hi, o_lo = split(full)
        own3[...] = jnp.concatenate([o_hi, o_lo, o_hi], axis=0)
        for dr, dc in SLOTS:
            if (dr, dc) != (0, 0):
                sky_copy(cyc, dr, dc).wait_recv()
        for dr, dc in SLOTS:
            c_hi, c_lo = split(
                sky_buf[cyc, (dr + 1) * 3 + dc + 1] * (scale * valid(dr, dc))
            )
            coef3[dr + 1, :, (dc + 1) * 128 : (dc + 2) * 128] = jnp.concatenate(
                [c_hi, c_lo, c_hi], axis=0
            )
        win[...] = jnp.zeros_like(win)

        def level(j, carry):
            for tr, (src, n, dst) in enumerate(
                ((half, half, 0), (0, tile, half), (0, half, half + tile))
            ):
                hi, lo = split(dot(left[j, src : src + n, :], coef3[tr]))
                u_hi[dst : dst + n, :] = hi
                u_lo[dst : dst + n, :] = lo
            at = pl.multiple_of(me * slab, slab)
            e_hi, e_lo = split(dot(left[j, pl.ds(at, slab), :], own3[...]))
            cut = [GAIN * jnp.abs(weights[k]) * thr_ref[j, k] for k in range(3)]
            raw = [thr_ref[j, k] for k in range(3)]

            def spread(hi, lo, h):
                c_hi = right[j, 0:128, 384 * h : 384 * (h + 1)]
                c_lo = right[j, 128:256, 384 * h : 384 * (h + 1)]
                return data_const(hi, lo, c_hi, c_lo)

            for h in range(2):
                got = spread(
                    jnp.concatenate([u_hi[:, 128:256], e_hi], axis=0),
                    jnp.concatenate([u_lo[:, 128:256], e_lo], axis=0),
                    h,
                )
                new = win[:, half * (1 + h) : half * (2 + h)]
                for k in range(3):
                    block = got[:, 128 * k : 128 * (k + 1)]
                    new = new + soft(block[: 2 * tile], cut[k])
                    model_out[k, :, half * h : half * (h + 1)] += GAIN * soft(
                        block[2 * tile :], raw[k]
                    )
                win[:, half * (1 + h) : half * (2 + h)] = new
            for side in range(2):
                lanes = slice(256 * side, 256 * side + 128)
                got = spread(u_hi[:, lanes], u_lo[:, lanes], 1 - side)
                cols = slice(3 * half * side, 3 * half * side + half)
                new = win[:, cols]
                for k in range(3):
                    new = new + soft(got[:, 128 * k : 128 * (k + 1)], cut[k])
                win[:, cols] = new
            return carry

        lax.fori_loop(0, levels, level, 0)

        for rb in range(4):
            tr, qr = ((-1, 1), (0, 0), (0, 1), (1, 0))[rb]
            for cb in range(4):
                tc, qc = ((-1, 1), (0, 0), (0, 1), (1, 0))[cb]
                at = FLAG_ROW + 2 * qr + qc
                flag = sky_buf[cyc, (tr + 1) * 3 + tc + 1, at : at + 1, :]
                rows, cols = slice(half * rb, half * (rb + 1)), slice(half * cb, half * (cb + 1))
                hi, lo = split(win[rows, cols] * flag)
                win_hi[rows, cols] = hi
                win_lo[rows, cols] = lo

        spec = const_data(rows_fwd[0], rows_fwd[1], win_hi[...], win_lo[...])
        near, far = spec[:, :tile], spec[:, tile:]
        for parity, v in enumerate((near + far, near - far)):
            hi, lo = split(v)
            sd_hi[parity] = hi
            sd_lo[parity] = lo

        @pl.when(cyc == 0)
        def _():
            copies[6].wait()
            copies[7].wait()

        z_acc[...] = jnp.zeros_like(z_acc)

        def column(parity, carry):
            hi, lo = rotate(sd_hi[parity], sd_lo[parity])
            x = data_const(hi, lo, cols_fwd[parity, 0], cols_fwd[parity, 1])
            x_re, x_im = x[:tile], x[tile:]
            b_re, b_im = beam_f[parity, :tile], beam_f[parity, tile:]
            y_re = x_re * b_re - x_im * b_im
            y_im = x_re * b_im + x_im * b_re
            r_hi, r_lo = split(y_re)
            i_hi, i_lo = split(y_im)

            def stack(re, im):
                return jnp.concatenate(
                    [jnp.concatenate([re, -im], axis=1), jnp.concatenate([im, re], axis=1)],
                    axis=0,
                )

            z_acc[...] += data_const(
                stack(r_hi, i_hi), stack(r_lo, i_lo), cols_inv[parity, 0], cols_inv[parity, 1]
            )
            return carry

        lax.fori_loop(0, 2, column, 0)
        z_hi, z_lo = split(z_acc[...])
        res_out[...] = res_out[...] - const_data(rows_inv[0], rows_inv[1], z_hi, z_lo)
        for d in range(1, bands):
            band_copy(cyc, d).wait_send()
        for dr, dc in SLOTS:
            if (dr, dc) != (0, 0):
                sky_copy(cyc, dr, dc).wait_send()
        return carry

    lax.fori_loop(0, CYCLES, cycle, 0)


def on_device(residual_start, beam_pattern, spec_weights, thresholds, block_ids, block_counts):
    bands = lax.axis_size("band")
    sky = lax.axis_size("sky")
    tile = residual_start.shape[-1]
    coefs = spec_weights.shape[1]
    levels = thresholds.shape[0]
    tables = host_tables(tile, levels)
    smem = pl.BlockSpec(memory_space=pltpu.SMEM)
    vmem = pl.BlockSpec(memory_space=pltpu.VMEM)
    hbm = pl.BlockSpec(memory_space=pl.ANY)
    region = 2 * tile
    model, res = pl.pallas_call(
        functools.partial(kernel, bands, sky),
        out_shape=(
            jax.ShapeDtypeStruct((coefs, tile // bands, tile), F32),
            jax.ShapeDtypeStruct((tile, tile), F32),
        ),
        in_specs=[smem] * 4 + [vmem] * 2 + [hbm] * 8,
        out_specs=(vmem, vmem),
        scratch_shapes=[pltpu.VMEM(t.shape, BF) for t in tables]
        + [
            pltpu.VMEM((CYCLES, bands, 16, 128), F32),
            pltpu.VMEM((CYCLES, 9, KPAD, 128), F32),
            pltpu.VMEM((3, 3 * KPAD, 384), BF),
            pltpu.VMEM((3 * KPAD, 128), BF),
            pltpu.VMEM((region, 384), BF),
            pltpu.VMEM((region, 384), BF),
            pltpu.VMEM((region, region), F32),
            pltpu.VMEM((region, region), BF),
            pltpu.VMEM((region, region), BF),
            pltpu.VMEM((2, region, tile), F32),
            pltpu.VMEM((2, region, tile), BF),
            pltpu.VMEM((2, region, tile), BF),
            pltpu.VMEM((region, tile), F32),
            pltpu.SemaphoreType.DMA((8,)),
            pltpu.SemaphoreType.DMA((CYCLES, bands)),
            pltpu.SemaphoreType.DMA((CYCLES, bands)),
            pltpu.SemaphoreType.DMA((CYCLES, 9)),
            pltpu.SemaphoreType.DMA((CYCLES, 9)),
        ],
        compiler_params=pltpu.CompilerParams(
            collective_id=0, has_side_effects=True, vmem_limit_bytes=56 << 20
        ),
    )(
        block_ids[0, 0],
        block_counts[0],
        spec_weights,
        thresholds,
        residual_start[0, 0],
        beam_pattern[0],
        *[jnp.asarray(t) for t in tables],
    )
    return (model[:, None], res[None, None])


def solution(mesh):
    placed = (
        P("band", "sky", None, None),
        P("band", None, None),
        P(),
        P(),
        P("band", "sky", None),
        P("band", "sky"),
    )
    return jax.shard_map(
        on_device,
        mesh=mesh,
        in_specs=placed,
        out_specs=(P(None, "sky", "band", None), P("band", "sky", None, None)),
        check_vma=False,
    )
```

time: 620 us -> 68.3 us (0.11)
  the two profiles are of different devices: /device:TPU:6 before, /device:TPU:1 now
where the time goes in v1:
time: 68.3 us; the launch traced here: 68.1 us
  Pallas kernels  62.3 us (91%)
  local copies, waits for them, and re-layouts  4.56 us (7%)
  between operations  1.29 us (2%)
    pallas_call x1, Pallas kernels, on_device(): pl.pallas_call(functools.partial(kernel, bands, sky), out_shape=(jax.Shap...  62.3 us
    unnamed x3, local copies, waits for them, and re-layouts  4.56 us

profile of v1, /device:TPU:1, one launch (start us, length us, event | category | flops | bytes accessed | tf_op | source)
XLA Modules:
  0.0 68.1 jit_solution(98320113874262118)
XLA Ops:
  1.3 1.3 %copy.16.weight_ref = f32[8,3]{1,0:T(8,128)} copy(f32[8,3]{0,1:T(4,128)} %param.16) | data formatting | bytes 192 | tf_op args[2]
  2.6 62.3 %shard_map.149 = (f32[3,32,256]{2,1,0:T(8,128)}, f32[256,256]{1,0:T(8,128)}) custom-call(s32[4]{0:T(128)} %bitcast.13, s32[1]{0:T(128)} %bitcast.8.count_ref, f32[8,3]{1,0:T(8,128)} %copy.16.weight_ref, f32[4,3]{1,0:T(4,128)} %thr_ref.1, f32[256,256]{1,0:T(8,128)} %bitcast.9, f32[256,256]{1,0:T(8,128)} %bitcast.10, ...), custom_call_target="tpu_custom_call" | custom-call | tf_op jit(solution)/shard_map/pallas_call | solution.py:439
  64.9 1.5 %copy.21 = f32[3,1,32,256]{3,2,1,0:T(8,128)} copy(f32[3,1,32,256]{3,2,1,0:T(8,128)} %bitcast.12) | data formatting | bytes 196608
  66.5 1.7 %copy.22 = f32[1,1,256,256]{3,2,1,0:T(8,128)} copy(f32[1,1,256,256]{3,2,1,0:T(8,128)} %bitcast.11) | data formatting | bytes 524288

commit v2 on v1

v2 whole, which is shorter than its diff:
```python
import functools

import jax
import jax.numpy as jnp
import numpy as np
from jax import lax
from jax.experimental import pallas as pl
from jax.experimental.pallas import tpu as pltpu
from jax.sharding import PartitionSpec as P

CYCLES = 2
TGX = 4
GAIN = 0.25
RANK = 42
KPAD = 48
FLAG_ROW = 44
MESH = pl.DeviceIdType.MESH
BF = jnp.bfloat16
F32 = jnp.float32


def host_split(a):
    hi = np.asarray(a, np.float64).astype(BF)
    lo = (np.asarray(a, np.float64) - hi.astype(np.float64)).astype(BF)
    return hi, lo


def host_tables(tile, levels):
    pos = np.arange(tile, dtype=np.float64)
    off = pos[:, None] - pos[None, :]
    smooth = []
    for j in range(levels):
        spread = 2.0**j * tile / 16.0
        k = np.exp(-off * off / (2.0 * spread * spread))
        smooth.append(k / np.sqrt(np.sum(k * k, axis=1, keepdims=True)))
    smooth = np.stack(smooth)
    _, _, vt = np.linalg.svd(smooth.reshape(-1, tile), full_matrices=False)
    basis = vt[:RANK].T
    proj = np.zeros((tile, 128))
    proj[:, :RANK] = basis
    proj_t = np.zeros((KPAD, tile))
    proj_t[:RANK] = basis.T
    expand = smooth @ basis

    p_hi, p_lo = host_split(proj)
    t_hi, t_lo = host_split(proj_t)
    project = np.concatenate([p_hi, p_hi, p_lo], axis=0)
    project_t = np.concatenate([t_hi, t_hi, t_lo], axis=1)

    left = np.zeros((levels, tile, KPAD))
    left[:, :, :RANK] = expand
    l_hi, l_lo = host_split(left)
    left3 = np.concatenate([l_hi, l_hi, l_lo], axis=2)

    right = np.zeros((levels, 128, tile), BF)
    g_hi, g_lo = host_split(expand.transpose(0, 2, 1))
    for p, g in enumerate((g_hi, g_hi, g_lo)):
        right[:, RANK * p : RANK * (p + 1)] = g

    n = 2 * tile
    f = np.arange(tile) + 0.5
    ang = 2.0 * np.pi * f[:, None] * np.arange(tile)[None, :] / n
    rows_fwd = np.stack(host_split(np.concatenate([np.cos(ang), -np.sin(ang)], axis=0)))

    fwd = []
    x = np.arange(tile)
    for parity in range(2):
        a = 2.0 * np.pi * x[:, None] * (2 * x[None, :] + parity) / n
        fwd.append(np.stack(host_split(np.concatenate([np.cos(a), np.sin(a)], axis=0))))
    cols_fwd = np.stack(fwd)
    return project_t, project, rows_fwd, cols_fwd, left3, right


def split(v):
    hi = v.astype(BF)
    return hi, (v - hi.astype(F32)).astype(BF)


def dot(a, b):
    return jnp.dot(a, b, preferred_element_type=F32)


def data_const(hi, lo, c_hi, c_lo):
    return dot(jnp.concatenate([hi, lo, hi], axis=1), jnp.concatenate([c_hi, c_hi, c_lo], axis=0))


def const_data(c_hi, c_lo, hi, lo):
    return dot(jnp.concatenate([c_hi, c_hi, c_lo], axis=1), jnp.concatenate([hi, lo, hi], axis=0))


def soft(v, t):
    return v - jnp.minimum(jnp.maximum(v, -t), t)


def rotate(hi, lo):
    half = hi.shape[0] // 2

    def one(v):
        return jnp.concatenate(
            [
                jnp.concatenate([v[:half], v[half:]], axis=1),
                jnp.concatenate([v[half:], -v[:half]], axis=1),
            ],
            axis=0,
        )

    return one(hi), one(lo)


NEAR = [(0, 1), (0, -1)]
FAR = [(1, 0), (-1, 0), (1, 1), (1, -1), (-1, 1), (-1, -1)]


def kernel(
    bands,
    sky,
    ids_ref,
    count_ref,
    weight_ref,
    thr_ref,
    res_in,
    beam_hbm,
    project_t_hbm,
    project_hbm,
    rows_hbm,
    cols_hbm,
    left_hbm,
    right_hbm,
    model_out,
    res_out,
    beam,
    project_t,
    project,
    rows_half,
    cols_fwd,
    left,
    right,
    rows_fwd,
    rows_inv,
    cols_odd,
    gather,
    sky_buf,
    coef3,
    own3,
    win,
    spec,
    beam_f,
    sd_hi,
    sd_lo,
    z_acc,
    const_sem,
    band_send,
    band_recv,
    sky_send,
    sky_recv,
):
    tile = res_in.shape[0]
    half = tile // 2
    levels = left.shape[0]
    slab = tile // bands
    sky_rows = sky // TGX
    me = lax.axis_index("band")
    spot = lax.axis_index("sky")
    row, col = spot // TGX, spot % TGX

    def sky_id(dr, dc):
        return ((row + dr + sky_rows) % sky_rows) * TGX + (col + dc + TGX) % TGX

    pairs = [
        (project_t_hbm, project_t),
        (project_hbm, project),
        (beam_hbm, beam),
        (rows_hbm, rows_half),
        (cols_hbm, cols_fwd),
        (left_hbm, left),
        (right_hbm, right),
    ]
    copies = [
        pltpu.make_async_copy(src, dst, const_sem.at[i]) for i, (src, dst) in enumerate(pairs)
    ]
    for copy in copies:
        copy.start()

    barrier = pltpu.get_barrier_semaphore()
    for d in range(1, bands):
        pl.semaphore_signal(
            barrier, inc=1, device_id={"band": (me + d) % bands}, device_id_type=MESH
        )
    for dr, dc in NEAR + FAR:
        pl.semaphore_signal(barrier, inc=1, device_id={"sky": sky_id(dr, dc)}, device_id_type=MESH)

    res_out[...] = res_in[...]
    model_out[...] = jnp.zeros_like(model_out)

    lane = lax.broadcasted_iota(jnp.int32, (1, 128), 1)
    lane16 = lax.broadcasted_iota(jnp.int32, (16, 128), 1)
    row48 = lax.broadcasted_iota(jnp.int32, (KPAD, 128), 0)
    flags = []
    for q in range(4):
        live = jnp.float32(0.0)
        for s in range(4):
            hit = jnp.where(ids_ref[s] == q, 1.0, 0.0) * jnp.where(s < count_ref[0], 1.0, 0.0)
            live = live + hit
        flags.append(live)
    weights = [weight_ref[k, me] for k in range(3)]
    scale = jnp.zeros((1, 128), F32)
    for k in range(3):
        inside = (lane >= RANK * k) & (lane < RANK * (k + 1))
        scale = jnp.where(inside, GAIN * weights[k], scale)

    def band_copy(cyc, d):
        return pltpu.make_async_remote_copy(
            src_ref=gather.at[cyc, 0],
            dst_ref=gather.at[cyc, d],
            send_sem=band_send.at[cyc, d],
            recv_sem=band_recv.at[cyc, d],
            device_id={"band": (me + d) % bands},
            device_id_type=MESH,
        )

    def sky_copy(cyc, dr, dc):
        slot = (1 - dr) * 3 + (1 - dc)
        return pltpu.make_async_remote_copy(
            src_ref=sky_buf.at[cyc, 4],
            dst_ref=sky_buf.at[cyc, slot],
            send_sem=sky_send.at[cyc, slot],
            recv_sem=sky_recv.at[cyc, slot],
            device_id={"sky": sky_id(dr, dc)},
            device_id_type=MESH,
        )

    def valid(dr, dc):
        good = (row + dr >= 0) & (row + dr < sky_rows) & (col + dc >= 0) & (col + dc < TGX)
        return jnp.where(good, 1.0, 0.0)

    def prepare():
        for copy in copies[2:5]:
            copy.wait()
        alt = (1 - 2 * (lax.broadcasted_iota(jnp.int32, (tile, 1), 0) % 2)).astype(F32)
        for part in range(2):
            re = rows_half[part, :tile].astype(F32)
            im = rows_half[part, tile:].astype(F32)
            re_far, im_far = im * alt, -(re * alt)
            rows_fwd[part, :, :tile] = rows_half[part]
            rows_fwd[part, :tile, tile:] = re_far.astype(BF)
            rows_fwd[part, tile:, tile:] = im_far.astype(BF)
            rows_inv[part, :, :tile] = re_far.T.astype(BF)
            rows_inv[part, :, tile:] = im_far.T.astype(BF)
            cols_odd[0, part] = cols_fwd[0, part]
            for h in range(2):
                block = cols_fwd[1, part, h * tile : (h + 1) * tile].astype(F32)
                cols_odd[1, part, h * tile : (h + 1) * tile] = (-block.T).astype(BF)
        b_hi, b_lo = split(beam[...])
        l_hi, l_lo = rotate(*split(const_data(rows_half[0], rows_half[1], b_hi, b_lo)))
        norm = 2.0 / (4 * tile * tile)
        for parity in range(2):
            got = data_const(l_hi, l_lo, cols_fwd[parity, 0], cols_fwd[parity, 1])
            beam_f[parity] = norm * got
        copies[5].wait()
        copies[6].wait()

    def place(cyc, dr, dc):
        c_hi, c_lo = split(sky_buf[cyc, (dr + 1) * 3 + dc + 1] * (scale * valid(dr, dc)))
        coef3[dr + 1, :, (dc + 1) * 128 : (dc + 2) * 128] = jnp.concatenate(
            [c_hi, c_lo, c_hi], axis=0
        )

    def expand(v):
        lanes = lax.broadcasted_iota(jnp.int32, v.shape, 1)
        hi = v.astype(BF).astype(F32)
        lo = v - hi

        def moved(x, by):
            return x if by == 0 else pltpu.roll(x, by % 128, 1)

        out = []
        for k in range(3):
            low = moved(hi, -RANK * k)
            mid = moved(lo, RANK - RANK * k)
            top = moved(hi, 2 * RANK - RANK * k)
            out.append(
                jnp.where(lanes < RANK, low, jnp.where(lanes < 2 * RANK, mid, top)).astype(BF)
            )
        return out

    def smooth(phase, groups):
        win[phase] = jnp.zeros(win.shape[1:], F32)

        def level(j, carry):
            first = jnp.concatenate(
                [dot(left[j, src : src + n, :], coef3[tr]) for src, n, tr in groups], axis=0
            )
            west, mid, east = (expand(first[:, 128 * t : 128 * (t + 1)]) for t in range(3))
            table = right[j]
            blank = jnp.zeros((128, half), BF)
            both = jnp.concatenate(
                [
                    jnp.concatenate([table[:, half:], blank], axis=1),
                    jnp.concatenate([blank, table[:, :half]], axis=1),
                ],
                axis=0,
            )
            cut = [GAIN * jnp.abs(weights[k]) * thr_ref[j, k] for k in range(3)]
            if phase == 0:
                at = pl.multiple_of(me * slab, slab)
                mid = mid + expand(dot(left[j, pl.ds(at, slab), :], own3[...]))
            got = dot(jnp.concatenate(mid, axis=0), table)
            new = win[phase, :, :tile]
            for k in range(3):
                new = new + soft(got[tile * k : tile * (k + 1)], cut[k])
            win[phase, :, :tile] = new
            if phase == 0:
                for k in range(3):
                    block = got[3 * tile + slab * k : 3 * tile + slab * (k + 1)]
                    model_out[k] += GAIN * soft(block, thr_ref[j, k])
            pairs = [jnp.concatenate([west[k], east[k]], axis=1) for k in range(3)]
            got = dot(jnp.concatenate(pairs, axis=0), both)
            new = win[phase, :, tile:]
            for k in range(3):
                new = new + soft(got[tile * k : tile * (k + 1)], cut[k])
            win[phase, :, tile:] = new
            return carry

        lax.fori_loop(0, levels, level, 0)

    def masked(cyc, phase, bands_of_rows):
        rows = []
        for at, (dr, qr) in enumerate(bands_of_rows):
            cols = []
            for (dc, qc), src in (((-1, 1), tile), ((0, 0), 0), ((0, 1), half), ((1, 0), tile + half)):
                f = FLAG_ROW + 2 * qr + qc
                flag = sky_buf[cyc, (dr + 1) * 3 + dc + 1, f : f + 1, :]
                cols.append(win[phase, half * at : half * (at + 1), src : src + half] * flag)
            rows.append(jnp.concatenate(cols, axis=1))
        return split(jnp.concatenate(rows, axis=0))

    def cycle(cyc, carry):
        r_hi, r_lo = split(res_out[...])
        part = dot(project_t[...], jnp.concatenate([r_hi, r_lo, r_hi], axis=0))
        p_hi, p_lo = split(part)
        coef = dot(jnp.concatenate([p_hi, p_lo, p_hi], axis=1), project[...])
        gather[cyc, 0] = (
            coef[0:16] + pltpu.roll(coef[16:32], RANK, 1) + pltpu.roll(coef[32:48], 2 * RANK, 1)
        )

        for d in range(1, bands):
            band_copy(cyc, d).start()

        @pl.when(cyc == 0)
        def _():
            prepare()

        for d in range(1, bands):
            band_copy(cyc, d).wait_recv()
        sums = []
        for k in range(3):
            total = weights[k] * gather[cyc, 0]
            for d in range(1, bands):
                total = total + weight_ref[k, (me - d + bands) % bands] * gather[cyc, d]
            sums.append(total)
        groups = []
        for g in range(3):
            out = jnp.zeros((16, 128), F32)
            for k in range(3):
                moved = sums[k]
                if k != g:
                    moved = pltpu.roll(moved, (RANK * (k - g)) % 128, 1)
                inside = (lane16 >= RANK * k) & (lane16 < RANK * (k + 1))
                out = jnp.where(inside, moved, out)
            groups.append(out)
        full = jnp.concatenate(groups, axis=0)
        for q in range(4):
            full = jnp.where(row48 == FLAG_ROW + q, flags[q], full)
        sky_buf[cyc, 4] = full
        for dr, dc in FAR + NEAR:
            sky_copy(cyc, dr, dc).start()

        o_hi, o_lo = split(full)
        own3[...] = jnp.concatenate([o_hi, o_lo, o_hi], axis=0)
        place(cyc, 0, 0)
        for dr, dc in NEAR:
            sky_copy(cyc, -dr, -dc).wait_recv()
            place(cyc, dr, dc)
        smooth(0, [(0, tile, 1)])
        w_hi, w_lo = masked(cyc, 0, [(0, 0), (0, 1)])
        inner = slice(half, half + tile)
        spec[...] = const_data(rows_fwd[0, :, inner], rows_fwd[1, :, inner], w_hi, w_lo)

        for dr, dc in FAR:
            sky_copy(cyc, -dr, -dc).wait_recv()
            place(cyc, dr, dc)
        smooth(1, [(half, half, 0), (0, half, 2)])
        w_hi, w_lo = masked(cyc, 1, [(-1, 1), (1, 0)])

        def outer(part):
            return jnp.concatenate(
                [rows_fwd[part, :, :half], rows_fwd[part, :, half + tile :]], axis=1
            )

        full_spec = spec[...] + const_data(outer(0), outer(1), w_hi, w_lo)
        near, far = full_spec[:, :tile], full_spec[:, tile:]
        for parity, v in enumerate((near + far, near - far)):
            hi, lo = split(v)
            sd_hi[parity] = hi
            sd_lo[parity] = lo

        z_acc[...] = jnp.zeros_like(z_acc)

        def column(parity, carry):
            hi, lo = rotate(sd_hi[parity], sd_lo[parity])
            x = data_const(hi, lo, cols_fwd[parity, 0], cols_fwd[parity, 1])
            x_re, x_im = x[:tile], x[tile:]
            b_re, b_im = beam_f[parity, :tile], beam_f[parity, tile:]
            y_re = x_re * b_re - x_im * b_im
            y_im = x_re * b_im + x_im * b_re
            r_hi, r_lo = split(y_re)
            i_hi, i_lo = split(y_im)

            def stack(re, im):
                return jnp.concatenate(
                    [jnp.concatenate([re, -im], axis=1), jnp.concatenate([im, re], axis=1)],
                    axis=0,
                )

            z_acc[...] += data_const(
                stack(r_hi, i_hi), stack(r_lo, i_lo), cols_odd[parity, 0], cols_odd[parity, 1]
            )
            return carry

        lax.fori_loop(0, 2, column, 0)
        z_hi, z_lo = split(z_acc[...])
        res_out[...] = res_out[...] - const_data(rows_inv[0], rows_inv[1], z_hi, z_lo)
        for d in range(1, bands):
            band_copy(cyc, d).wait_send()
        for dr, dc in NEAR + FAR:
            sky_copy(cyc, dr, dc).wait_send()
        return carry

    copies[0].wait()
    copies[1].wait()
    pl.semaphore_wait(barrier, bands - 1 + 8)
    lax.fori_loop(0, CYCLES, cycle, 0)


def finish(model_in, res_in, model_out, res_out):
    model_out[...] = model_in[...]
    res_out[...] = res_in[...]


def on_device(residual_start, beam_pattern, spec_weights, thresholds, block_ids, block_counts):
    bands = lax.axis_size("band")
    sky = lax.axis_size("sky")
    tile = residual_start.shape[-1]
    coefs = spec_weights.shape[1]
    levels = thresholds.shape[0]
    tables = host_tables(tile, levels)
    smem = pl.BlockSpec(memory_space=pltpu.SMEM)
    vmem = pl.BlockSpec(memory_space=pltpu.VMEM)
    hbm = pl.BlockSpec(memory_space=pl.ANY)
    region = 2 * tile
    shapes = (
        jax.ShapeDtypeStruct((coefs, tile // bands, tile), F32),
        jax.ShapeDtypeStruct((tile, tile), F32),
    )
    model, res = pl.pallas_call(
        functools.partial(kernel, bands, sky),
        out_shape=shapes,
        in_specs=[smem] * 4 + [vmem] + [hbm] * 7,
        out_specs=(vmem, vmem),
        scratch_shapes=[pltpu.VMEM((tile, tile), F32)]
        + [pltpu.VMEM(t.shape, BF) for t in tables]
        + [
            pltpu.VMEM((2, region, region), BF),
            pltpu.VMEM((2, tile, region), BF),
            pltpu.VMEM((2, 2, region, tile), BF),
            pltpu.VMEM((CYCLES, bands, 16, 128), F32),
            pltpu.VMEM((CYCLES, 9, KPAD, 128), F32),
            pltpu.VMEM((3, 3 * KPAD, 384), BF),
            pltpu.VMEM((3 * KPAD, 128), BF),
            pltpu.VMEM((2, tile, region), F32),
            pltpu.VMEM((region, region), F32),
            pltpu.VMEM((2, region, tile), F32),
            pltpu.VMEM((2, region, tile), BF),
            pltpu.VMEM((2, region, tile), BF),
            pltpu.VMEM((region, tile), F32),
            pltpu.SemaphoreType.DMA((7,)),
            pltpu.SemaphoreType.DMA((CYCLES, bands)),
            pltpu.SemaphoreType.DMA((CYCLES, bands)),
            pltpu.SemaphoreType.DMA((CYCLES, 9)),
            pltpu.SemaphoreType.DMA((CYCLES, 9)),
        ],
        compiler_params=pltpu.CompilerParams(
            collective_id=0, has_side_effects=True, vmem_limit_bytes=32 << 20
        ),
    )(
        block_ids[0, 0],
        block_counts[0],
        spec_weights.T,
        thresholds,
        *[
            pltpu.with_memory_space_constraint(x, pltpu.HBM)
            for x in (
                residual_start[0, 0],
                beam_pattern[0],
                *[jnp.asarray(t) for t in tables],
            )
        ],
    )
    model, res = pl.pallas_call(
        finish,
        out_shape=shapes,
        in_specs=[vmem] * 2,
        out_specs=(vmem, vmem),
        compiler_params=pltpu.CompilerParams(vmem_limit_bytes=4 << 20),
    )(model, res)
    return (model[:, None], res[None, None])


def solution(mesh):
    placed = (
        P("band", "sky", None, None),
        P("band", None, None),
        P(),
        P(),
        P("band", "sky", None),
        P("band", "sky"),
    )
    return jax.shard_map(
        on_device,
        mesh=mesh,
        in_specs=placed,
        out_specs=(P(None, "sky", "band", None), P("band", "sky", None, None)),
        check_vma=False,
    )
```

time: 68.3 us -> 58.7 us (0.86); the launches traced: 68.1 us -> 57.8 us
  Pallas kernels: 62.3 us -> 55.8 us
  local copies, waits for them, and re-layouts: 4.56 us -> 0.68 us
    pallas_call x1 -> x2, Pallas kernels: 62.3 us -> 55.8 us  [the longest x1 55 us: on_device(): pl.pallas_call(functools.partial(kernel, bands, sky), out_shape=shapes, i...]
    unnamed x3 -> x6, local copies, waits for them, and re-layouts: 4.56 us -> 0.68 us
where the time goes in v2:
time: 58.7 us; the launch traced here: 57.8 us
  Pallas kernels  55.8 us (95%)
  between operations  1.31 us (2%)
  local copies, waits for them, and re-layouts  0.68 us (1%)
    pallas_call x1, Pallas kernels, on_device(): pl.pallas_call(functools.partial(kernel, bands, sky), out_shape=shapes, i...  55 us

profile of v2, /device:TPU:1, one launch (start us, length us, event | category | flops | bytes accessed | tf_op | source)
XLA Modules:
  0.0 57.8 jit_solution(6512836914607082911)
XLA Ops:
  1.3 0.0 copy-start.1
  1.3 0.0 copy-start
  1.3 0.0 copy-start.2
  1.3 0.7 %copy-done.1 = f32[4,3]{1,0:T(4,128)S(1)} copy-done((f32[4,3]{1,0:T(4,128)S(1)}, f32[4,3]{1,0:T(4,128)}, u32[]{:S(2)}) %copy-start.1) | copy-done | bytes 72
  2.0 0.0 copy-done
  2.0 0.0 copy-done.2
  2.0 55.0 %shard_map.131 = (f32[3,32,256]{2,1,0:T(8,128)S(1)}, f32[256,256]{1,0:T(8,128)S(1)}) custom-call(s32[4]{0:T(128)S(1)} %bitcast.11, s32[1]{0:T(128)} %bitcast.9.count_ref, f32[3,8]{1,0:T(4,128)S(1)} %bitcast.10, f32[4,3]{1,0:T(4,128)S(1)} %copy-done.1, f32[256,256]{1,0:T(8,128)} %bitcast.12, f32[256,256]{1,0:T(8,128)} %bitcast.13, ...), custom_call_target="tpu_custom_call" | custom-call | tf_op jit(solution)/shard_map/pallas_call | solution.py:465
  57.0 0.8 %shard_map.132 = (f32[3,32,256]{2,1,0:T(8,128)}, f32[256,256]{1,0:T(8,128)}) custom-call(f32[3,32,256]{2,1,0:T(8,128)S(1)} %get-tuple-element.6.model_in, f32[256,256]{1,0:T(8,128)S(1)} %get-tuple-element.7.res_in), custom_call_target="tpu_custom_call" | custom-call | tf_op jit(solution)/shard_map/pallas_call | solution.py:509
Async XLA Ops:
  1.3 0.7 %copy-start.1 = (f32[4,3]{1,0:T(4,128)S(1)}, f32[4,3]{1,0:T(4,128)}, u32[]{:S(2)}) copy-start(f32[4,3]{1,0:T(4,128)} %thr_ref.1) | copy-start | bytes 148
  1.3 0.7 %copy-start = (f32[8,3]{0,1:T(4,128)S(1)}, f32[8,3]{0,1:T(4,128)}, u32[]{:S(2)}) copy-start(f32[8,3]{0,1:T(4,128)} %param.14) | copy-start | bytes 292
  1.3 0.7 %copy-start.2 = (s32[1,1,4]{2,1,0:T(1,128)S(1)}, s32[1,1,4]{2,1,0:T(1,128)}, u32[]{:S(2)}) copy-start(s32[1,1,4]{2,1,0:T(1,128)} %param.16) | copy-start | bytes 52

commit v3 on v2

v3 whole, which is shorter than its diff:
```python
import functools

import jax
import jax.numpy as jnp
import numpy as np
from jax import lax
from jax.experimental import pallas as pl
from jax.experimental.pallas import tpu as pltpu
from jax.sharding import PartitionSpec as P

CYCLES = 2
TGX = 4
GAIN = 0.25
RANK = 42
KPAD = 48
FAR_RANK = 32
MESH = pl.DeviceIdType.MESH
BF = jnp.bfloat16
F32 = jnp.float32


def host_split(a):
    hi = np.asarray(a, np.float64).astype(BF)
    lo = (np.asarray(a, np.float64) - hi.astype(np.float64)).astype(BF)
    return hi, lo


def host_tables(tile, levels):
    pos = np.arange(tile, dtype=np.float64)
    off = pos[:, None] - pos[None, :]
    smooth = []
    for j in range(levels):
        spread = 2.0**j * tile / 16.0
        k = np.exp(-off * off / (2.0 * spread * spread))
        smooth.append(k / np.sqrt(np.sum(k * k, axis=1, keepdims=True)))
    smooth = np.stack(smooth)
    _, _, vt = np.linalg.svd(smooth.reshape(-1, tile), full_matrices=False)
    basis = vt[:RANK].T
    proj = np.zeros((tile, 128))
    proj[:, :RANK] = basis
    proj_t = np.zeros((KPAD, tile))
    proj_t[:RANK] = basis.T
    expand = smooth @ basis

    p_hi, p_lo = host_split(proj)
    t_hi, t_lo = host_split(proj_t)
    project = np.concatenate([p_hi, p_hi, p_lo], axis=0)
    project_t = np.concatenate([t_hi, t_hi, t_lo], axis=1)

    left = np.zeros((levels, tile, KPAD))
    left[:, :, :RANK] = expand
    l_hi, l_lo = host_split(left)
    left3 = np.concatenate([l_hi, l_hi, l_lo], axis=2)

    far, reduce = [], np.zeros((2 * FAR_RANK, KPAD))
    for i, rows in enumerate((slice(tile // 2, tile), slice(0, tile // 2))):
        _, _, vt = np.linalg.svd(expand[:, rows].reshape(-1, RANK), full_matrices=False)
        reduce[FAR_RANK * i : FAR_RANK * (i + 1), :RANK] = vt[:FAR_RANK]
        f_hi, f_lo = host_split(expand[:, rows] @ vt[:FAR_RANK].T)
        far.append(np.concatenate([f_hi, f_hi, f_lo], axis=2))
    left_far = np.stack(far, axis=1)
    z_hi, z_lo = host_split(reduce)
    reduce3 = np.concatenate([z_hi, z_hi, z_lo], axis=1)

    right = np.zeros((levels, 128, tile), BF)
    g_hi, g_lo = host_split(expand.transpose(0, 2, 1))
    for p, g in enumerate((g_hi, g_hi, g_lo)):
        right[:, RANK * p : RANK * (p + 1)] = g

    n = 2 * tile
    f = np.arange(tile) + 0.5
    ang = 2.0 * np.pi * f[:, None] * np.arange(tile)[None, :] / n
    rows_fwd = np.stack(host_split(np.concatenate([np.cos(ang), -np.sin(ang)], axis=0)))

    cols = []
    x = np.arange(tile // 2)
    for r in range(4):
        a = 2.0 * np.pi * x[:, None] * (4 * x[None, :] + r) / n
        c, s = np.cos(a), np.sin(a)
        cols.append(np.stack(host_split(np.block([[c, -s], [s, c]]))))
    cols = np.stack(cols)
    return project_t, project, reduce3, rows_fwd, cols, left3, right, left_far


def split(v):
    hi = v.astype(BF)
    return hi, (v - hi.astype(F32)).astype(BF)


def dot(a, b):
    return jnp.dot(a, b, preferred_element_type=F32)


def data_const(hi, lo, c_hi, c_lo):
    return dot(jnp.concatenate([hi, lo, hi], axis=1), jnp.concatenate([c_hi, c_hi, c_lo], axis=0))


def const_data(c_hi, c_lo, hi, lo):
    return dot(jnp.concatenate([c_hi, c_hi, c_lo], axis=1), jnp.concatenate([hi, lo, hi], axis=0))


def soft(v, t):
    return v - jnp.minimum(jnp.maximum(v, -t), t)


def residues(re, im):
    (a_re, b_re, c_re, d_re), (a_im, b_im, c_im, d_im) = (
        (v[0] + v[2], v[1] + v[3], v[0] - v[2], v[1] - v[3]) for v in (re, im)
    )
    return [
        jnp.concatenate(pair, axis=1)
        for pair in (
            (a_re + b_re, a_im + b_im),
            (c_re + d_im, c_im - d_re),
            (a_re - b_re, a_im - b_im),
            (c_re - d_im, c_im + d_re),
        )
    ]


NEAR = [(0, 1), (0, -1)]
FAR = [(1, 0), (-1, 0), (1, 1), (1, -1), (-1, 1), (-1, -1)]


def kernel(
    bands,
    sky,
    ids_ref,
    count_ref,
    weight_ref,
    thr_ref,
    res_in,
    beam_hbm,
    project_t_hbm,
    project_hbm,
    reduce_hbm,
    rows_hbm,
    cols_hbm,
    left_hbm,
    right_hbm,
    left_far_hbm,
    model_out,
    res_out,
    beam,
    project_t,
    project,
    reduce,
    rows_half,
    cols,
    left,
    right,
    left_far,
    rows_fwd,
    rows_inv,
    cols_t,
    gather,
    sky_buf,
    far_out,
    far_in,
    coef3,
    far3,
    own3,
    win,
    spec,
    beam_f,
    const_sem,
    band_send,
    band_recv,
    sky_send,
    sky_recv,
):
    tile = res_in.shape[0]
    half = tile // 2
    levels = left.shape[0]
    slab = tile // bands
    sky_rows = sky // TGX
    me = lax.axis_index("band")
    spot = lax.axis_index("sky")
    row, col = spot // TGX, spot % TGX

    def sky_id(dr, dc):
        return ((row + dr + sky_rows) % sky_rows) * TGX + (col + dc + TGX) % TGX

    pairs = [
        (project_t_hbm, project_t),
        (project_hbm, project),
        (beam_hbm, beam),
        (rows_hbm, rows_half),
        (cols_hbm, cols),
        (reduce_hbm, reduce),
        (left_hbm, left),
        (right_hbm, right),
        (left_far_hbm, left_far),
    ]
    copies = [
        pltpu.make_async_copy(src, dst, const_sem.at[i]) for i, (src, dst) in enumerate(pairs)
    ]
    for copy in copies:
        copy.start()

    barrier = pltpu.get_barrier_semaphore()
    for d in range(1, bands):
        pl.semaphore_signal(
            barrier, inc=1, device_id={"band": (me + d) % bands}, device_id_type=MESH
        )
    for dr, dc in NEAR + FAR:
        pl.semaphore_signal(barrier, inc=1, device_id={"sky": sky_id(dr, dc)}, device_id_type=MESH)

    res_out[...] = res_in[...]
    model_out[...] = jnp.zeros_like(model_out)

    lane = lax.broadcasted_iota(jnp.int32, (1, 128), 1)
    lane16 = lax.broadcasted_iota(jnp.int32, (16, 128), 1)
    flags = []
    for q in range(4):
        live = jnp.float32(0.0)
        for s in range(4):
            hit = jnp.where(ids_ref[s] == q, 1.0, 0.0) * jnp.where(s < count_ref[0], 1.0, 0.0)
            live = live + hit
        flags.append(live)
    weights = [weight_ref[k, me] for k in range(3)]
    scale = jnp.zeros((1, 128), F32)
    for k in range(3):
        ours = (lane >= RANK * k) & (lane < RANK * (k + 1))
        scale = jnp.where(ours, GAIN * weights[k], scale)

    def band_copy(cyc, d):
        return pltpu.make_async_remote_copy(
            src_ref=gather.at[cyc, 0],
            dst_ref=gather.at[cyc, d],
            send_sem=band_send.at[cyc, d],
            recv_sem=band_recv.at[cyc, d],
            device_id={"band": (me + d) % bands},
            device_id_type=MESH,
        )

    def near_slot(dc):
        return (dc + 3) % 3

    def sky_copy(cyc, dr, dc):
        if dr == 0:
            src, dst = sky_buf.at[cyc, 0], sky_buf.at[cyc, near_slot(-dc)]
        else:
            src, dst = far_out.at[cyc, (1 - dr) // 2], far_in.at[cyc, far_slot(-dr, -dc)]
        slot = (1 - dr) * 3 + (1 - dc)
        return pltpu.make_async_remote_copy(
            src_ref=src,
            dst_ref=dst,
            send_sem=sky_send.at[cyc, slot],
            recv_sem=sky_recv.at[cyc, slot],
            device_id={"sky": sky_id(dr, dc)},
            device_id_type=MESH,
        )

    def far_slot(dr, dc):
        return (dr + 1) // 2 * 3 + dc + 1

    def inside(dr, dc):
        return (row + dr >= 0) & (row + dr < sky_rows) & (col + dc >= 0) & (col + dc < TGX)

    for dr, dc in NEAR + FAR:

        @pl.when(jnp.logical_not(inside(dr, dc)))
        def _():
            for cyc in range(CYCLES):
                if dr == 0:
                    sky_buf[cyc, near_slot(dc)] = jnp.zeros((KPAD, 128), F32)
                else:
                    far_in[cyc, far_slot(dr, dc)] = jnp.zeros((FAR_RANK, 128), F32)

    def send(cyc, where):
        for dr, dc in where:

            @pl.when(inside(dr, dc))
            def _():
                sky_copy(cyc, dr, dc).start()

    def receive(cyc, where):
        for dr, dc in where:

            @pl.when(inside(dr, dc))
            def _():
                sky_copy(cyc, -dr, -dc).wait_recv()

    def with_flags(v):
        r = lax.broadcasted_iota(jnp.int32, v.shape, 0)
        c = lax.broadcasted_iota(jnp.int32, v.shape, 1)
        for q in range(4):
            v = jnp.where((c == 127) & (r == q), flags[q], v)
        return v

    def prepare():
        for copy in copies[2:5]:
            copy.wait()
        alt = (1 - 2 * (lax.broadcasted_iota(jnp.int32, (tile, 1), 0) % 2)).astype(F32)
        b_hi, b_lo = split(beam[...])
        first = const_data(rows_half[0], rows_half[1], b_hi, b_lo)
        blank = jnp.zeros((tile, half), F32)
        re, im = (
            [first[at : at + tile, :half], first[at : at + tile, half:], blank, blank]
            for at in (0, tile)
        )
        norm = 2.0 / (4 * tile * tile)
        for r, v in enumerate(residues(re, im)):
            hi, lo = split(v)
            beam_f[r] = norm * data_const(hi, lo, cols[r, 0], cols[r, 1])
        for part in range(2):
            re = rows_half[part, :tile].astype(F32)
            im = rows_half[part, tile:].astype(F32)
            re_far, im_far = im * alt, -(re * alt)
            rows_fwd[part, :, :tile] = rows_half[part]
            rows_fwd[part, :tile, tile:] = re_far.astype(BF)
            rows_fwd[part, tile:, tile:] = im_far.astype(BF)
            rows_inv[part, :, :tile] = re_far.T.astype(BF)
            rows_inv[part, :, tile:] = im_far.T.astype(BF)
            for r in range(4):
                cols_t[r, part] = cols[r, part].astype(F32).T.astype(BF)
        for copy in copies[5:]:
            copy.wait()

    def place(dst, lanes, v):
        hi, lo = split(v * scale)
        dst[:, 128 * lanes : 128 * (lanes + 1)] = jnp.concatenate([hi, lo, hi], axis=0)

    def expand(v):
        lanes = lax.broadcasted_iota(jnp.int32, v.shape, 1)
        hi, lo = split(v)

        def moved(x, by):
            return x if by == 0 else pltpu.roll(x, by % 128, 1)

        out = []
        for k in range(3):
            low = moved(hi, -RANK * k)
            mid = moved(lo, RANK - RANK * k)
            top = moved(hi, 2 * RANK - RANK * k)
            out.append(jnp.where(lanes < RANK, low, jnp.where(lanes < 2 * RANK, mid, top)))
        return out

    def smooth(phase):
        chunk = half // 2
        blank = jnp.zeros((128, half), BF)

        def pack(j, c):
            rows = slice(chunk * c, chunk * (c + 1))
            if phase == 0:
                first = dot(left[j, rows, :], coef3[...])
            else:
                rows = slice(chunk * (c % 2), chunk * (c % 2 + 1))
                first = dot(left_far[j, c // 2, rows, :], far3[c // 2])
            west, mid, east = (expand(first[:, 128 * t : 128 * (t + 1)]) for t in range(3))
            pairs = [jnp.concatenate([west[k], east[k]], axis=1) for k in range(3)]
            return jnp.concatenate(mid, axis=0), jnp.concatenate(pairs, axis=0)

        def add(j, c, mid, pairs):
            rows = slice(chunk * c, chunk * (c + 1))
            table = right[j]
            both = jnp.concatenate(
                [
                    jnp.concatenate([table[:, half:], blank], axis=1),
                    jnp.concatenate([blank, table[:, :half]], axis=1),
                ],
                axis=0,
            )
            for at, got in ((0, dot(mid, table)), (tile, dot(pairs, both))):
                new = None if j == 0 else win[phase, rows, at : at + tile]
                for k in range(3):
                    cut = GAIN * jnp.abs(weights[k]) * thr_ref[j, k]
                    term = soft(got[chunk * k : chunk * (k + 1)], cut)
                    new = term if new is None else new + term
                win[phase, rows, at : at + tile] = new

        def model(j):
            at = pl.multiple_of(me * slab, slab)
            mine = expand(dot(left[j, pl.ds(at, slab), :], own3[...]))
            got = dot(jnp.concatenate(mine, axis=0), right[j])
            for k in range(3):
                term = GAIN * soft(got[slab * k : slab * (k + 1)], thr_ref[j, k])
                model_out[k] += term

        packed = {}
        for step in range(levels + 1):
            for c in range(4):
                if step < levels:
                    packed[step, c] = pack(step, c)
                if step > 0:
                    add(step - 1, c, *packed.pop((step - 1, c)))
            if phase == 0 and step < levels:
                model(step)

    def masked(cyc, phase, bands_of_rows):
        rows = []
        for at, (dr, qr) in enumerate(bands_of_rows):
            blocks = []
            for (dc, qc), src in (((-1, 1), tile), ((0, 0), 0), ((0, 1), half), ((1, 0), tile + half)):
                q = 2 * qr + qc
                if dr == 0:
                    flag = sky_buf[cyc, near_slot(dc), q : q + 1, 127:128]
                else:
                    flag = far_in[cyc, far_slot(dr, dc), q : q + 1, 127:128]
                blocks.append(win[phase, half * at : half * (at + 1), src : src + half] * flag)
            rows.append(jnp.concatenate(blocks, axis=1))
        return split(jnp.concatenate(rows, axis=0))

    def cycle(cyc, carry):
        r_hi, r_lo = split(res_out[...])
        part = dot(project_t[...], jnp.concatenate([r_hi, r_lo, r_hi], axis=0))
        p_hi, p_lo = split(part)
        coef = dot(jnp.concatenate([p_hi, p_lo, p_hi], axis=1), project[...])
        gather[cyc, 0] = (
            coef[0:16] + pltpu.roll(coef[16:32], RANK, 1) + pltpu.roll(coef[32:48], 2 * RANK, 1)
        )

        for d in range(1, bands):
            band_copy(cyc, d).start()

        @pl.when(cyc == 0)
        def _():
            prepare()

        for d in range(1, bands):
            band_copy(cyc, d).wait_recv()
        sums = []
        for k in range(3):
            total = weights[k] * gather[cyc, 0]
            for d in range(1, bands):
                total = total + weight_ref[k, (me - d + bands) % bands] * gather[cyc, d]
            sums.append(total)
        groups = []
        for g in range(3):
            out = jnp.zeros((16, 128), F32)
            for k in range(3):
                moved = sums[k]
                if k != g:
                    moved = pltpu.roll(moved, (RANK * (k - g)) % 128, 1)
                ours = (lane16 >= RANK * k) & (lane16 < RANK * (k + 1))
                out = jnp.where(ours, moved, out)
            groups.append(out)
        full = jnp.concatenate(groups, axis=0)
        o_hi, o_lo = split(full)
        stacked = jnp.concatenate([o_hi, o_lo, o_hi], axis=0)
        less = dot(reduce[...], stacked)
        for i in range(2):
            far_out[cyc, i] = with_flags(less[FAR_RANK * i : FAR_RANK * (i + 1)])
        send(cyc, FAR)
        sky_buf[cyc, 0] = with_flags(full)
        send(cyc, NEAR)
        own3[...] = stacked
        place(coef3, 1, full)
        receive(cyc, NEAR)
        for dr, dc in NEAR:
            place(coef3, dc + 1, sky_buf[cyc, near_slot(dc)])
        smooth(0)
        w_hi, w_lo = masked(cyc, 0, [(0, 0), (0, 1)])
        inner = slice(half, half + tile)
        spec[...] = const_data(rows_fwd[0, :, inner], rows_fwd[1, :, inner], w_hi, w_lo)

        receive(cyc, FAR)
        for dr, dc in FAR:
            place(far3.at[(dr + 1) // 2], dc + 1, far_in[cyc, far_slot(dr, dc)])
        smooth(1)
        w_hi, w_lo = masked(cyc, 1, [(-1, 1), (1, 0)])

        def outer(part):
            return jnp.concatenate(
                [rows_fwd[part, :, :half], rows_fwd[part, :, half + tile :]], axis=1
            )

        full_spec = spec[...] + const_data(outer(0), outer(1), w_hi, w_lo)
        re, im = (
            [full_spec[at : at + tile, half * m : half * (m + 1)] for m in range(4)]
            for at in (0, tile)
        )
        back = []
        for r, v in enumerate(residues(re, im)):
            hi, lo = split(v)
            x = data_const(hi, lo, cols[r, 0], cols[r, 1])
            x_re, x_im = x[:, :half], x[:, half:]
            b_re, b_im = beam_f[r, :, :half], beam_f[r, :, half:]
            hi, lo = split(
                jnp.concatenate([x_re * b_re - x_im * b_im, x_re * b_im + x_im * b_re], axis=1)
            )
            back.append(data_const(hi, lo, cols_t[r, 0], cols_t[r, 1]))
        even, odd = back[0] + back[2], back[1] + back[3]
        gap, turn = back[0] - back[2], back[1] - back[3]
        z_re = jnp.concatenate(
            [even[:, :half] - odd[:, :half], gap[:, :half] + turn[:, half:]], axis=1
        )
        z_im = jnp.concatenate(
            [even[:, half:] - odd[:, half:], gap[:, half:] - turn[:, :half]], axis=1
        )
        z_hi, z_lo = split(jnp.concatenate([z_re, z_im], axis=0))
        res_out[...] = res_out[...] - const_data(rows_inv[0], rows_inv[1], z_hi, z_lo)
        for d in range(1, bands):
            band_copy(cyc, d).wait_send()
        for dr, dc in NEAR + FAR:

            @pl.when(inside(dr, dc))
            def _():
                sky_copy(cyc, dr, dc).wait_send()

        return carry

    copies[0].wait()
    copies[1].wait()
    pl.semaphore_wait(barrier, bands - 1 + 8)
    lax.fori_loop(0, CYCLES, cycle, 0)


def finish(model_in, res_in, model_out, res_out):
    model_out[...] = model_in[...]
    res_out[...] = res_in[...]


def on_device(residual_start, beam_pattern, spec_weights, thresholds, block_ids, block_counts):
    bands = lax.axis_size("band")
    sky = lax.axis_size("sky")
    tile = residual_start.shape[-1]
    coefs = spec_weights.shape[1]
    levels = thresholds.shape[0]
    tables = host_tables(tile, levels)
    smem = pl.BlockSpec(memory_space=pltpu.SMEM)
    vmem = pl.BlockSpec(memory_space=pltpu.VMEM)
    hbm = pl.BlockSpec(memory_space=pl.ANY)
    region = 2 * tile
    shapes = (
        jax.ShapeDtypeStruct((coefs, tile // bands, tile), F32),
        jax.ShapeDtypeStruct((tile, tile), F32),
    )
    model, res = pl.pallas_call(
        functools.partial(kernel, bands, sky),
        out_shape=shapes,
        in_specs=[smem] * 4 + [vmem] + [hbm] * 9,
        out_specs=(vmem, vmem),
        scratch_shapes=[pltpu.VMEM((tile, tile), F32)]
        + [pltpu.VMEM(t.shape, BF) for t in tables]
        + [
            pltpu.VMEM((2, region, region), BF),
            pltpu.VMEM((2, tile, region), BF),
            pltpu.VMEM((4, 2, tile, tile), BF),
            pltpu.VMEM((CYCLES, bands, 16, 128), F32),
            pltpu.VMEM((CYCLES, 3, KPAD, 128), F32),
            pltpu.VMEM((CYCLES, 2, FAR_RANK, 128), F32),
            pltpu.VMEM((CYCLES, 6, FAR_RANK, 128), F32),
            pltpu.VMEM((3 * KPAD, 384), BF),
            pltpu.VMEM((2, 3 * FAR_RANK, 384), BF),
            pltpu.VMEM((3 * KPAD, 128), BF),
            pltpu.VMEM((2, tile, region), F32),
            pltpu.VMEM((region, region), F32),
            pltpu.VMEM((4, tile, tile), F32),
            pltpu.SemaphoreType.DMA((9,)),
            pltpu.SemaphoreType.DMA((CYCLES, bands)),
            pltpu.SemaphoreType.DMA((CYCLES, bands)),
            pltpu.SemaphoreType.DMA((CYCLES, 9)),
            pltpu.SemaphoreType.DMA((CYCLES, 9)),
        ],
        compiler_params=pltpu.CompilerParams(
            collective_id=0, has_side_effects=True, vmem_limit_bytes=32 << 20
        ),
    )(
        block_ids[0, 0],
        block_counts[0],
        spec_weights.T,
        thresholds,
        *[
            pltpu.with_memory_space_constraint(x, pltpu.HBM)
            for x in (
                residual_start[0, 0],
                beam_pattern[0],
                *[jnp.asarray(t) for t in tables],
            )
        ],
    )
    model, res = pl.pallas_call(
        finish,
        out_shape=shapes,
        in_specs=[vmem] * 2,
        out_specs=(vmem, vmem),
        compiler_params=pltpu.CompilerParams(vmem_limit_bytes=4 << 20),
    )(model, res)
    return (model[:, None], res[None, None])


def solution(mesh):
    placed = (
        P("band", "sky", None, None),
        P("band", None, None),
        P(),
        P(),
        P("band", "sky", None),
        P("band", "sky"),
    )
    return jax.shard_map(
        on_device,
        mesh=mesh,
        in_specs=placed,
        out_specs=(P(None, "sky", "band", None), P("band", "sky", None, None)),
        check_vma=False,
    )
```

time: 58.7 us -> 45.4 us (0.77); the launches traced: 57.8 us -> 45.3 us
  Pallas kernels: 55.8 us -> 43.3 us
    pallas_call x1, Pallas kernels: 55 us -> 42.5 us  [on_device(): pl.pallas_call(functools.partial(kernel, bands, sky), out_shape=shapes, i...]
where the time goes in v3:
time: 45.4 us; the launch traced here: 45.3 us
  Pallas kernels  43.3 us (95%)
  between operations  1.31 us (3%)
  local copies, waits for them, and re-layouts  0.68 us (1%)
    pallas_call x1, Pallas kernels, on_device(): pl.pallas_call(functools.partial(kernel, bands, sky), out_shape=shapes, i...  42.5 us

profile of v3, /device:TPU:1, one launch (start us, length us, event | category | flops | bytes accessed | tf_op | source)
XLA Modules:
  0.0 45.3 jit_solution(15123423196690685527)
XLA Ops:
  1.3 0.0 copy-start.1
  1.3 0.0 copy-start
  1.3 0.0 copy-start.2
  1.3 0.7 %copy-done.1 = f32[4,3]{1,0:T(4,128)S(1)} copy-done((f32[4,3]{1,0:T(4,128)S(1)}, f32[4,3]{1,0:T(4,128)}, u32[]{:S(2)}) %copy-start.1) | copy-done | bytes 72
  2.0 0.0 copy-done
  2.0 0.0 copy-done.2
  2.0 42.5 %shard_map.149 = (f32[3,32,256]{2,1,0:T(8,128)S(1)}, f32[256,256]{1,0:T(8,128)S(1)}) custom-call(s32[4]{0:T(128)S(1)} %bitcast.11, s32[1]{0:T(128)} %bitcast.9.count_ref, f32[3,8]{1,0:T(4,128)S(1)} %bitcast.10, f32[4,3]{1,0:T(4,128)S(1)} %copy-done.1, f32[256,256]{1,0:T(8,128)} %bitcast.12, f32[256,256]{1,0:T(8,128)} %bitcast.13, ...), custom_call_target="tpu_custom_call" | custom-call | tf_op jit(solution)/shard_map/pallas_call | solution.py:530
  44.5 0.8 %shard_map.150 = (f32[3,32,256]{2,1,0:T(8,128)}, f32[256,256]{1,0:T(8,128)}) custom-call(f32[3,32,256]{2,1,0:T(8,128)S(1)} %get-tuple-element.6.model_in, f32[256,256]{1,0:T(8,128)S(1)} %get-tuple-element.7.res_in), custom_call_target="tpu_custom_call" | custom-call | tf_op jit(solution)/shard_map/pallas_call | solution.py:574
Async XLA Ops:
  1.3 0.7 %copy-start.1 = (f32[4,3]{1,0:T(4,128)S(1)}, f32[4,3]{1,0:T(4,128)}, u32[]{:S(2)}) copy-start(f32[4,3]{1,0:T(4,128)} %thr_ref.1) | copy-start | bytes 148
  1.3 0.7 %copy-start = (f32[8,3]{0,1:T(4,128)S(1)}, f32[8,3]{0,1:T(4,128)}, u32[]{:S(2)}) copy-start(f32[8,3]{0,1:T(4,128)} %param.16) | copy-start | bytes 292
  1.3 0.7 %copy-start.2 = (s32[1,1,4]{2,1,0:T(1,128)S(1)}, s32[1,1,4]{2,1,0:T(1,128)}, u32[]{:S(2)}) copy-start(s32[1,1,4]{2,1,0:T(1,128)} %param.18) | copy-start | bytes 52

commit v4 on v3

--- a/solution.py
+++ b/solution.py
@@ -125,11 +125,11 @@
 def kernel(
     bands,
     sky,
-    ids_ref,
-    count_ref,
-    weight_ref,
-    thr_ref,
-    res_in,
+    ids_hbm,
+    count_hbm,
+    weight_hbm,
+    thr_hbm,
+    res_hbm,
     beam_hbm,
     project_t_hbm,
     project_hbm,
@@ -141,6 +141,10 @@
     left_far_hbm,
     model_out,
     res_out,
+    ids_ref,
+    count_ref,
+    weight_ref,
+    thr_ref,
     beam,
     project_t,
     project,
@@ -169,7 +173,7 @@
     sky_send,
     sky_recv,
 ):
-    tile = res_in.shape[0]
+    tile = res_out.shape[0]
     half = tile // 2
     levels = left.shape[0]
     slab = tile // bands
@@ -182,6 +186,7 @@
         return ((row + dr + sky_rows) % sky_rows) * TGX + (col + dc + TGX) % TGX
 
     pairs = [
+        (res_hbm, res_out),
         (project_t_hbm, project_t),
         (project_hbm, project),
         (beam_hbm, beam),
@@ -191,11 +196,15 @@
         (left_hbm, left),
         (right_hbm, right),
         (left_far_hbm, left_far),
+        (ids_hbm, ids_ref),
+        (count_hbm, count_ref),
+        (weight_hbm, weight_ref),
+        (thr_hbm, thr_ref),
     ]
     copies = [
         pltpu.make_async_copy(src, dst, const_sem.at[i]) for i, (src, dst) in enumerate(pairs)
     ]
-    for copy in copies:
+    for copy in copies[:3]:
         copy.start()
 
     barrier = pltpu.get_barrier_semaphore()
@@ -206,11 +215,42 @@
     for dr, dc in NEAR + FAR:
         pl.semaphore_signal(barrier, inc=1, device_id={"sky": sky_id(dr, dc)}, device_id_type=MESH)
 
-    res_out[...] = res_in[...]
+    for copy in copies[3:]:
+        copy.start()
+
+    def band_copy(cyc, d):
+        return pltpu.make_async_remote_copy(
+            src_ref=gather.at[cyc, 0],
+            dst_ref=gather.at[cyc, d],
+            send_sem=band_send.at[cyc, d],
+            recv_sem=band_recv.at[cyc, d],
+            device_id={"band": (me + d) % bands},
+            device_id_type=MESH,
+        )
+
+    def compress(cyc):
+        r_hi, r_lo = split(res_out[...])
+        part = dot(project_t[...], jnp.concatenate([r_hi, r_lo, r_hi], axis=0))
+        p_hi, p_lo = split(part)
+        coef = dot(jnp.concatenate([p_hi, p_lo, p_hi], axis=1), project[...])
+        gather[cyc, 0] = (
+            coef[0:16] + pltpu.roll(coef[16:32], RANK, 1) + pltpu.roll(coef[32:48], 2 * RANK, 1)
+        )
+        if isinstance(cyc, int):
+            pl.semaphore_wait(barrier, bands - 1 + 8)
+        for d in range(1, bands):
+            band_copy(cyc, d).start()
+
+    for copy in copies[:3]:
+        copy.wait()
+    compress(0)
+
     model_out[...] = jnp.zeros_like(model_out)
 
     lane = lax.broadcasted_iota(jnp.int32, (1, 128), 1)
     lane16 = lax.broadcasted_iota(jnp.int32, (16, 128), 1)
+    for copy in copies[10:]:
+        copy.wait()
     flags = []
     for q in range(4):
         live = jnp.float32(0.0)
@@ -223,16 +263,6 @@
     for k in range(3):
         ours = (lane >= RANK * k) & (lane < RANK * (k + 1))
         scale = jnp.where(ours, GAIN * weights[k], scale)
-
-    def band_copy(cyc, d):
-        return pltpu.make_async_remote_copy(
-            src_ref=gather.at[cyc, 0],
-            dst_ref=gather.at[cyc, d],
-            send_sem=band_send.at[cyc, d],
-            recv_sem=band_recv.at[cyc, d],
-            device_id={"band": (me + d) % bands},
-            device_id_type=MESH,
-        )
 
     def near_slot(dc):
         return (dc + 3) % 3
@@ -290,7 +320,7 @@
         return v
 
     def prepare():
-        for copy in copies[2:5]:
+        for copy in copies[3:6]:
             copy.wait()
         alt = (1 - 2 * (lax.broadcasted_iota(jnp.int32, (tile, 1), 0) % 2)).astype(F32)
         b_hi, b_lo = split(beam[...])
@@ -315,8 +345,10 @@
             rows_inv[part, :, tile:] = im_far.T.astype(BF)
             for r in range(4):
                 cols_t[r, part] = cols[r, part].astype(F32).T.astype(BF)
-        for copy in copies[5:]:
+        for copy in copies[6:10]:
             copy.wait()
+
+    prepare()
 
     def place(dst, lanes, v):
         hi, lo = split(v * scale)
@@ -403,21 +435,6 @@
         return split(jnp.concatenate(rows, axis=0))
 
     def cycle(cyc, carry):
-        r_hi, r_lo = split(res_out[...])
-        part = dot(project_t[...], jnp.concatenate([r_hi, r_lo, r_hi], axis=0))
-        p_hi, p_lo = split(part)
-        coef = dot(jnp.concatenate([p_hi, p_lo, p_hi], axis=1), project[...])
-        gather[cyc, 0] = (
-            coef[0:16] + pltpu.roll(coef[16:32], RANK, 1) + pltpu.roll(coef[32:48], 2 * RANK, 1)
-        )
-
-        for d in range(1, bands):
-            band_copy(cyc, d).start()
-
-        @pl.when(cyc == 0)
-        def _():
-            prepare()
-
         for d in range(1, bands):
             band_copy(cyc, d).wait_recv()
         sums = []
@@ -461,28 +478,53 @@
         smooth(1)
         w_hi, w_lo = masked(cyc, 1, [(-1, 1), (1, 0)])
 
-        def outer(part):
-            return jnp.concatenate(
-                [rows_fwd[part, :, :half], rows_fwd[part, :, half + tile :]], axis=1
+        w_rows = jnp.concatenate([w_hi, w_lo, w_hi], axis=0)
+        part_rows = half
+
+        def freqs(c):
+            return [slice(at + part_rows * c, at + part_rows * (c + 1)) for at in (0, tile)]
+
+        def start(c):
+            def outer(part):
+                return jnp.concatenate(
+                    [
+                        jnp.concatenate(
+                            [rows_fwd[part, f, :half], rows_fwd[part, f, half + tile :]], axis=1
+                        )
+                        for f in freqs(c)
+                    ],
+                    axis=0,
+                )
+
+            hi = outer(0)
+            got = dot(jnp.concatenate([hi, hi, outer(1)], axis=1), w_rows)
+            re, im = (
+                got[part_rows * i : part_rows * (i + 1)] + spec[f, :]
+                for i, f in enumerate(freqs(c))
             )
-
-        full_spec = spec[...] + const_data(outer(0), outer(1), w_hi, w_lo)
-        re, im = (
-            [full_spec[at : at + tile, half * m : half * (m + 1)] for m in range(4)]
-            for at in (0, tile)
-        )
-        back = []
-        for r, v in enumerate(residues(re, im)):
-            hi, lo = split(v)
-            x = data_const(hi, lo, cols[r, 0], cols[r, 1])
+            blocks = [[v[:, half * m : half * (m + 1)] for m in range(4)] for v in (re, im)]
+            return [split(v) for v in residues(*blocks)]
+
+        def along(pair, r):
+            return data_const(*pair, cols[r, 0], cols[r, 1])
+
+        def back(r, x):
             x_re, x_im = x[:, :half], x[:, half:]
             b_re, b_im = beam_f[r, :, :half], beam_f[r, :, half:]
             hi, lo = split(
                 jnp.concatenate([x_re * b_re - x_im * b_im, x_re * b_im + x_im * b_re], axis=1)
             )
-            back.append(data_const(hi, lo, cols_t[r, 0], cols_t[r, 1]))
-        even, odd = back[0] + back[2], back[1] + back[3]
-        gap, turn = back[0] - back[2], back[1] - back[3]
+            return data_const(hi, lo, cols_t[r, 0], cols_t[r, 1])
+
+        first, second = start(0), start(1)
+        x, t = [], []
+        for r in range(4):
+            pair = [jnp.concatenate([first[r][i], second[r][i]], axis=0) for i in range(2)]
+            x.append(along(pair, r))
+            if r > 0:
+                t.append(back(r - 1, x[r - 1]))
+        t.append(back(3, x[3]))
+        even, odd, gap, turn = t[0] + t[2], t[1] + t[3], t[0] - t[2], t[1] - t[3]
         z_re = jnp.concatenate(
             [even[:, :half] - odd[:, :half], gap[:, :half] + turn[:, half:]], axis=1
         )
@@ -491,6 +533,15 @@
         )
         z_hi, z_lo = split(jnp.concatenate([z_re, z_im], axis=0))
         res_out[...] = res_out[...] - const_data(rows_inv[0], rows_inv[1], z_hi, z_lo)
+
+        @pl.when(cyc + 1 < CYCLES)
+        def _():
+            compress(cyc + 1)
+
+        return carry
+
+    lax.fori_loop(0, CYCLES, cycle, 0)
+    for cyc in range(CYCLES):
         for d in range(1, bands):
             band_copy(cyc, d).wait_send()
         for dr, dc in NEAR + FAR:
@@ -498,13 +549,6 @@
             @pl.when(inside(dr, dc))
             def _():
                 sky_copy(cyc, dr, dc).wait_send()
-
-        return carry
-
-    copies[0].wait()
-    copies[1].wait()
-    pl.semaphore_wait(barrier, bands - 1 + 8)
-    lax.fori_loop(0, CYCLES, cycle, 0)
 
 
 def finish(model_in, res_in, model_out, res_out):
@@ -519,7 +563,6 @@
     coefs = spec_weights.shape[1]
     levels = thresholds.shape[0]
     tables = host_tables(tile, levels)
-    smem = pl.BlockSpec(memory_space=pltpu.SMEM)
     vmem = pl.BlockSpec(memory_space=pltpu.VMEM)
     hbm = pl.BlockSpec(memory_space=pl.ANY)
     region = 2 * tile
@@ -530,9 +573,15 @@
     model, res = pl.pallas_call(
         functools.partial(kernel, bands, sky),
         out_shape=shapes,
-        in_specs=[smem] * 4 + [vmem] + [hbm] * 9,
+        in_specs=[hbm] * 14,
         out_specs=(vmem, vmem),
-        scratch_shapes=[pltpu.VMEM((tile, tile), F32)]
+        scratch_shapes=[
+            pltpu.SMEM((4,), jnp.int32),
+            pltpu.SMEM((1,), jnp.int32),
+            pltpu.SMEM((coefs, bands), F32),
+            pltpu.SMEM((levels, coefs), F32),
+            pltpu.VMEM((tile, tile), F32),
+        ]
         + [pltpu.VMEM(t.shape, BF) for t in tables]
         + [
             pltpu.VMEM((2, region, region), BF),
@@ -548,7 +597,7 @@
             pltpu.VMEM((2, tile, region), F32),
             pltpu.VMEM((region, region), F32),
             pltpu.VMEM((4, tile, tile), F32),
-            pltpu.SemaphoreType.DMA((9,)),
+            pltpu.SemaphoreType.DMA((14,)),
             pltpu.SemaphoreType.DMA((CYCLES, bands)),
             pltpu.SemaphoreType.DMA((CYCLES, bands)),
             pltpu.SemaphoreType.DMA((CYCLES, 9)),
@@ -558,13 +607,13 @@
             collective_id=0, has_side_effects=True, vmem_limit_bytes=32 << 20
         ),
     )(
-        block_ids[0, 0],
+        pltpu.with_memory_space_constraint(block_ids[0, 0], pltpu.HBM),
         block_counts[0],
-        spec_weights.T,
-        thresholds,
         *[
             pltpu.with_memory_space_constraint(x, pltpu.HBM)
             for x in (
+                spec_weights.T,
+                thresholds,
                 residual_start[0, 0],
                 beam_pattern[0],
                 *[jnp.asarray(t) for t in tables],

time: 45.4 us -> 43.1 us (0.949)
  Pallas kernels: 43.3 us -> 41.5 us
  local copies, waits for them, and re-layouts: 0.68 us -> 0 us
    pallas_call x1, Pallas kernels: 42.5 us -> 40.8 us  [on_device(): pl.pallas_call(functools.partial(kernel, bands, sky), out_shape=shapes, i...]
    unnamed x6 -> x0, local copies, waits for them, and re-layouts: 0.68 us -> none
where the time goes in v4:
time: 43.1 us; the launch traced here: 42.8 us
  Pallas kernels  41.5 us (96%)
  between operations  1.29 us (3%)
    pallas_call x1, Pallas kernels, on_device(): pl.pallas_call(functools.partial(kernel, bands, sky), out_shape=shapes, i...  40.8 us

profile of v4, /device:TPU:1, one launch (start us, length us, event | category | flops | bytes accessed | tf_op | source)
XLA Modules:
  0.0 42.8 jit_solution(2426612574811464368)
XLA Ops:
  1.3 40.8 %shard_map.149 = (f32[3,32,256]{2,1,0:T(8,128)S(1)}, f32[256,256]{1,0:T(8,128)S(1)}) custom-call(s32[4]{0:T(128)} %bitcast.13, s32[1]{0:T(128)} %bitcast.9.count_hbm, f32[3,8]{1,0:T(4,128)} %bitcast.12, f32[4,3]{1,0:T(4,128)} %thr_hbm.1, f32[256,256]{1,0:T(8,128)} %bitcast.10, f32[256,256]{1,0:T(8,128)} %bitcast.11, ...), custom_call_target="tpu_custom_call" | custom-call | tf_op jit(solution)/shard_map/pallas_call | solution.py:573
  42.0 0.8 %shard_map.150 = (f32[3,32,256]{2,1,0:T(8,128)}, f32[256,256]{1,0:T(8,128)}) custom-call(f32[3,32,256]{2,1,0:T(8,128)S(1)} %get-tuple-element.6.model_in, f32[256,256]{1,0:T(8,128)S(1)} %get-tuple-element.7.res_in), custom_call_target="tpu_custom_call" | custom-call | tf_op jit(solution)/shard_map/pallas_call | solution.py:623

commit v5 on v4

--- a/solution.py
+++ b/solution.py
@@ -119,7 +119,7 @@
 
 
 NEAR = [(0, 1), (0, -1)]
-FAR = [(1, 0), (-1, 0), (1, 1), (1, -1), (-1, 1), (-1, -1)]
+FAR = [(1, 0), (1, 1), (1, -1), (-1, 0), (-1, 1), (-1, -1)]
 
 
 def kernel(
@@ -238,7 +238,7 @@
         )
         if isinstance(cyc, int):
             pl.semaphore_wait(barrier, bands - 1 + 8)
-        for d in range(1, bands):
+        for d in sorted(range(1, bands), key=lambda d: -min(d // 2, (bands - d) // 2)):
             band_copy(cyc, d).start()
 
     for copy in copies[:3]:
@@ -369,7 +369,7 @@
             out.append(jnp.where(lanes < RANK, low, jnp.where(lanes < 2 * RANK, mid, top)))
         return out
 
-    def smooth(phase):
+    def smooth(phase, arrive):
         chunk = half // 2
         blank = jnp.zeros((128, half), BF)
 
@@ -410,13 +410,18 @@
                 term = GAIN * soft(got[slab * k : slab * (k + 1)], thr_ref[j, k])
                 model_out[k] += term
 
+        items = [(j, pair) for pair in ((0, 1), (2, 3)) for j in range(levels)]
         packed = {}
-        for step in range(levels + 1):
-            for c in range(4):
-                if step < levels:
-                    packed[step, c] = pack(step, c)
+        for step in range(len(items) + 1):
+            if step % levels == 0 and step < len(items):
+                arrive(step // levels)
+            for i in range(2):
+                if step < len(items):
+                    j, pair = items[step]
+                    packed[step, i] = pack(j, pair[i])
                 if step > 0:
-                    add(step - 1, c, *packed.pop((step - 1, c)))
+                    j, pair = items[step - 1]
+                    add(j, pair[i], *packed.pop((step - 1, i)))
             if phase == 0 and step < levels:
                 model(step)
 
@@ -467,15 +472,18 @@
         receive(cyc, NEAR)
         for dr, dc in NEAR:
             place(coef3, dc + 1, sky_buf[cyc, near_slot(dc)])
-        smooth(0)
+        smooth(0, lambda i: None)
         w_hi, w_lo = masked(cyc, 0, [(0, 0), (0, 1)])
         inner = slice(half, half + tile)
         spec[...] = const_data(rows_fwd[0, :, inner], rows_fwd[1, :, inner], w_hi, w_lo)
 
-        receive(cyc, FAR)
-        for dr, dc in FAR:
-            place(far3.at[(dr + 1) // 2], dc + 1, far_in[cyc, far_slot(dr, dc)])
-        smooth(1)
+        def arrive(i):
+            group = (FAR[3:], FAR[:3])[i]
+            receive(cyc, group)
+            for dr, dc in group:
+                place(far3.at[(dr + 1) // 2], dc + 1, far_in[cyc, far_slot(dr, dc)])
+
+        smooth(1, arrive)
         w_hi, w_lo = masked(cyc, 1, [(-1, 1), (1, 0)])
 
         w_rows = jnp.concatenate([w_hi, w_lo, w_hi], axis=0)

time: 43.1 us -> 44.4 us (1.030)
  Pallas kernels: 41.5 us -> 43 us
    pallas_call x1, Pallas kernels: 40.8 us -> 42.2 us  [on_device(): pl.pallas_call(functools.partial(kernel, bands, sky), out_shape=shapes, i...]
where the time goes in v5:
time: 44.4 us; the launch traced here: 44.3 us
  Pallas kernels  43 us (97%)
  between operations  1.29 us (3%)
    pallas_call x1, Pallas kernels, on_device(): pl.pallas_call(functools.partial(kernel, bands, sky), out_shape=shapes, i...  42.2 us

profile of v5, /device:TPU:1, one launch (start us, length us, event | category | flops | bytes accessed | tf_op | source)
XLA Modules:
  0.0 44.3 jit_solution(2583051898809543231)
XLA Ops:
  1.3 42.2 %shard_map.149 = (f32[3,32,256]{2,1,0:T(8,128)S(1)}, f32[256,256]{1,0:T(8,128)S(1)}) custom-call(s32[4]{0:T(128)} %bitcast.13, s32[1]{0:T(128)} %bitcast.9.count_hbm, f32[3,8]{1,0:T(4,128)} %bitcast.12, f32[4,3]{1,0:T(4,128)} %thr_hbm.1, f32[256,256]{1,0:T(8,128)} %bitcast.10, f32[256,256]{1,0:T(8,128)} %bitcast.11, ...), custom_call_target="tpu_custom_call" | custom-call | tf_op jit(solution)/shard_map/pallas_call | solution.py:581
  43.5 0.8 %shard_map.150 = (f32[3,32,256]{2,1,0:T(8,128)}, f32[256,256]{1,0:T(8,128)}) custom-call(f32[3,32,256]{2,1,0:T(8,128)S(1)} %get-tuple-element.6.model_in, f32[256,256]{1,0:T(8,128)S(1)} %get-tuple-element.7.res_in), custom_call_target="tpu_custom_call" | custom-call | tf_op jit(solution)/shard_map/pallas_call | solution.py:631

commit v6 on v4

--- a/solution.py
+++ b/solution.py
@@ -13,6 +13,7 @@
 GAIN = 0.25
 RANK = 42
 KPAD = 48
+AHEAD = 4
 FAR_RANK = 32
 MESH = pl.DeviceIdType.MESH
 BF = jnp.bfloat16
@@ -119,7 +120,7 @@
 
 
 NEAR = [(0, 1), (0, -1)]
-FAR = [(1, 0), (-1, 0), (1, 1), (1, -1), (-1, 1), (-1, -1)]
+FAR = [(1, 1), (1, -1), (1, 0), (-1, 0), (-1, 1), (-1, -1)]
 
 
 def kernel(
@@ -238,7 +239,7 @@
         )
         if isinstance(cyc, int):
             pl.semaphore_wait(barrier, bands - 1 + 8)
-        for d in range(1, bands):
+        for d in sorted(range(1, bands), key=lambda d: (-min(d // 2, (bands - d) // 2), d % 2)):
             band_copy(cyc, d).start()
 
     for copy in copies[:3]:
@@ -410,15 +411,16 @@
                 term = GAIN * soft(got[slab * k : slab * (k + 1)], thr_ref[j, k])
                 model_out[k] += term
 
+        items = [(j, c) for j in range(levels) for c in range(4)]
         packed = {}
-        for step in range(levels + 1):
-            for c in range(4):
-                if step < levels:
-                    packed[step, c] = pack(step, c)
-                if step > 0:
-                    add(step - 1, c, *packed.pop((step - 1, c)))
-            if phase == 0 and step < levels:
-                model(step)
+        for step in range(0, len(items) + AHEAD, AHEAD):
+            for i in range(step, step + AHEAD):
+                if i >= AHEAD:
+                    add(*items[i - AHEAD], *packed.pop(i - AHEAD))
+                if i < len(items):
+                    packed[i] = pack(*items[i])
+            if phase == 0 and step < AHEAD * levels and step % AHEAD == 0:
+                model(step // AHEAD)
 
     def masked(cyc, phase, bands_of_rows):
         rows = []

time: 43.1 us -> 43.2 us (level)
  no operation moved by 1% of the time
where the time goes in v6:
time: 43.2 us; the launch traced here: 43.1 us
  Pallas kernels  41.8 us (97%)
  between operations  1.29 us (3%)
    pallas_call x1, Pallas kernels, on_device(): pl.pallas_call(functools.partial(kernel, bands, sky), out_shape=shapes, i...  41 us

profile of v6, /device:TPU:1, one launch (start us, length us, event | category | flops | bytes accessed | tf_op | source)
XLA Modules:
  0.0 43.1 jit_solution(13347465564308767794)
XLA Ops:
  1.3 41.0 %shard_map.149 = (f32[3,32,256]{2,1,0:T(8,128)S(1)}, f32[256,256]{1,0:T(8,128)S(1)}) custom-call(s32[4]{0:T(128)} %bitcast.13, s32[1]{0:T(128)} %bitcast.9.count_hbm, f32[3,8]{1,0:T(4,128)} %bitcast.12, f32[4,3]{1,0:T(4,128)} %thr_hbm.1, f32[256,256]{1,0:T(8,128)} %bitcast.10, f32[256,256]{1,0:T(8,128)} %bitcast.11, ...), custom_call_target="tpu_custom_call" | custom-call | tf_op jit(solution)/shard_map/pallas_call | solution.py:575
  42.3 0.8 %shard_map.150 = (f32[3,32,256]{2,1,0:T(8,128)}, f32[256,256]{1,0:T(8,128)}) custom-call(f32[3,32,256]{2,1,0:T(8,128)S(1)} %get-tuple-element.6.model_in, f32[256,256]{1,0:T(8,128)S(1)} %get-tuple-element.7.res_in), custom_call_target="tpu_custom_call" | custom-call | tf_op jit(solution)/shard_map/pallas_call | solution.py:625

commit v7 on v6

--- a/solution.py
+++ b/solution.py
@@ -120,7 +120,7 @@
 
 
 NEAR = [(0, 1), (0, -1)]
-FAR = [(1, 1), (1, -1), (1, 0), (-1, 0), (-1, 1), (-1, -1)]
+FAR = [(1, 0), (-1, 0), (1, 1), (1, -1), (-1, 1), (-1, -1)]
 
 
 def kernel(
@@ -239,7 +239,7 @@
         )
         if isinstance(cyc, int):
             pl.semaphore_wait(barrier, bands - 1 + 8)
-        for d in sorted(range(1, bands), key=lambda d: (-min(d // 2, (bands - d) // 2), d % 2)):
+        for d in range(1, bands):
             band_copy(cyc, d).start()
 
     for copy in copies[:3]:

time: 43.2 us -> 43 us (level)
  no operation moved by 1% of the time
where the time goes in v7:
time: 43 us; the launch traced here: 42.9 us
  Pallas kernels  41.6 us (97%)
  between operations  1.29 us (3%)
    pallas_call x1, Pallas kernels, on_device(): pl.pallas_call(functools.partial(kernel, bands, sky), out_shape=shapes, i...  40.8 us

profile of v7, /device:TPU:1, one launch (start us, length us, event | category | flops | bytes accessed | tf_op | source)
XLA Modules:
  0.0 42.9 jit_solution(13506544143403529859)
XLA Ops:
  1.3 40.8 %shard_map.149 = (f32[3,32,256]{2,1,0:T(8,128)S(1)}, f32[256,256]{1,0:T(8,128)S(1)}) custom-call(s32[4]{0:T(128)} %bitcast.13, s32[1]{0:T(128)} %bitcast.9.count_hbm, f32[3,8]{1,0:T(4,128)} %bitcast.12, f32[4,3]{1,0:T(4,128)} %thr_hbm.1, f32[256,256]{1,0:T(8,128)} %bitcast.10, f32[256,256]{1,0:T(8,128)} %bitcast.11, ...), custom_call_target="tpu_custom_call" | custom-call | tf_op jit(solution)/shard_map/pallas_call | solution.py:575
  42.1 0.8 %shard_map.150 = (f32[3,32,256]{2,1,0:T(8,128)}, f32[256,256]{1,0:T(8,128)}) custom-call(f32[3,32,256]{2,1,0:T(8,128)S(1)} %get-tuple-element.6.model_in, f32[256,256]{1,0:T(8,128)S(1)} %get-tuple-element.7.res_in), custom_call_target="tpu_custom_call" | custom-call | tf_op jit(solution)/shard_map/pallas_call | solution.py:625

commit v8 on v7

--- a/solution.py
+++ b/solution.py
@@ -538,7 +538,7 @@
 
         @pl.when(cyc + 1 < CYCLES)
         def _():
-            compress(cyc + 1)
+            compress((cyc + 1) % CYCLES)
 
         return carry
 

time: 43 us -> 43 us (level)
  no operation moved by 1% of the time
where the time goes in v8:
time: 43 us; the launch traced here: 42.9 us
  Pallas kernels  41.6 us (97%)
  between operations  1.29 us (3%)
    pallas_call x1, Pallas kernels, on_device(): pl.pallas_call(functools.partial(kernel, bands, sky), out_shape=shapes, i...  40.8 us

profile of v8, /device:TPU:1, one launch (start us, length us, event | category | flops | bytes accessed | tf_op | source)
XLA Modules:
  0.0 42.9 jit_solution(14022341927928992423)
XLA Ops:
  1.3 40.8 %shard_map.149 = (f32[3,32,256]{2,1,0:T(8,128)S(1)}, f32[256,256]{1,0:T(8,128)S(1)}) custom-call(s32[4]{0:T(128)} %bitcast.13, s32[1]{0:T(128)} %bitcast.9.count_hbm, f32[3,8]{1,0:T(4,128)} %bitcast.12, f32[4,3]{1,0:T(4,128)} %thr_hbm.1, f32[256,256]{1,0:T(8,128)} %bitcast.10, f32[256,256]{1,0:T(8,128)} %bitcast.11, ...), custom_call_target="tpu_custom_call" | custom-call | tf_op jit(solution)/shard_map/pallas_call | solution.py:575
  42.1 0.8 %shard_map.150 = (f32[3,32,256]{2,1,0:T(8,128)}, f32[256,256]{1,0:T(8,128)}) custom-call(f32[3,32,256]{2,1,0:T(8,128)S(1)} %get-tuple-element.6.model_in, f32[256,256]{1,0:T(8,128)S(1)} %get-tuple-element.7.res_in), custom_call_target="tpu_custom_call" | custom-call | tf_op jit(solution)/shard_map/pallas_call | solution.py:625
